TPU v7x, 512 devices: a whole 4x4x16 slice. The times are simulated.
512 devices in a mesh: lat: 64 (over z, y), wid: 2 (over core), tok: 4 (over x).
Axes of the slice: x: 4, y: 4, z: 16, core: 2. Of those that a mesh axis runs over, the one named last changes fastest.
Arguments:
- resid: bfloat16 [512, 4096], P('tok', 'wid'), may hold values from -6 to 6
- dictionary: bfloat16 [32768, 4096], P('lat', 'wid'), may hold values from -0.1875 to 0.1875
- enc_bias: float32 [32768], P('lat'), may hold values from -3 to 3
- dec_bias: float32 [4096], P('wid'), may hold values from -3 to 3
- active_blocks: int32 [512, 8], P('tok'), may hold values from 0 to 255, all different within a row
- level_bounds: int32 [4], replicated, may hold values from 1 to 256, as said below
Outputs:
- level_losses: float32 [4], replicated
- dict_grad: bfloat16 [4096, 32768], P(('wid', 'tok'), 'lat')
Inputs may be any that keep to these rules, and one draw needn't show every extreme that they name: `active_blocks`: each row names 8 different blocks. `level_bounds`: strictly increasing; the last equals 256.
All inputs are finite; a program needn't handle non-finite values.
Results may differ from a plain program's by a relative error of at most 0.006.
Values sent between devices are 32-bit elements; how exact they have to be, the bound alone decides.
A program may use at most 192 MiB of HBM per device.

v0:
```python
import jax
import jax.numpy as jnp
from jax import lax
from jax.sharding import PartitionSpec as P

LEVELS = 4


def entering(part, axis, combine, identity):
    place = lax.axis_index(axis)
    gathered = lax.all_gather(part, axis)
    state = jnp.zeros_like(part) + jnp.asarray(identity, part.dtype)

    def one(turn, state):
        return combine(state, lax.dynamic_index_in_dim(gathered, turn, 0, False))

    return lax.fori_loop(0, place, one, state)


def broadcast(array, axis, root):
    mine = lax.axis_index(axis) == root
    return lax.psum(jnp.where(mine, array, jnp.zeros_like(array)), axis)


def gelu_tanh(value):
    return jax.nn.gelu(value, approximate=True)


def add_pair(earlier, later):
    return earlier + later


def body(resid, dictionary, enc_bias, dec_bias, active_blocks, level_bounds):
    row_count, half_width = resid.shape
    lat_count = dictionary.shape[0]
    blocks_here = lat_count // 128
    lat_position = lax.axis_index("lat")
    first_block = lat_position * blocks_here
    local_ids = first_block + jnp.arange(blocks_here, dtype=jnp.int32)
    resid_full = resid.astype(jnp.float32)
    dict_blocks = dictionary.reshape(blocks_here, 128, half_width)
    partial_pre = lax.dot_general(
        resid, dictionary, (((1,), (1,)), ((), ())), preferred_element_type=jnp.float32
    )
    pre = lax.psum(partial_pre, "wid") + enc_bias[None, :]
    hits = jnp.any(active_blocks[:, :, None] == local_ids[None, None, :], axis=1).astype(
        jnp.float32
    )
    act = (gelu_tanh(pre).reshape(row_count, blocks_here, 128) * hits[:, :, None]).astype(
        jnp.bfloat16
    )
    act_flat = act.reshape(row_count, lat_count)
    latent_block = jnp.arange(lat_count, dtype=jnp.int32) // 128
    owners = []
    keeps = []
    for level in range(LEVELS):
        bound = level_bounds[level]
        owners.append((bound - 1) // blocks_here)
        inside = jnp.clip(bound - 1 - first_block, 0, blocks_here - 1)
        keeps.append(latent_block <= inside)
    keeps.append(latent_block >= 0)
    keep_rows = jnp.stack(keeps)
    act_stack = jnp.where(keep_rows[:, None, :], act_flat[None], jnp.zeros((), jnp.bfloat16))
    partials = jnp.dot(
        act_stack.reshape((LEVELS + 1) * row_count, lat_count),
        dictionary,
        preferred_element_type=jnp.float32,
    )
    partials = partials.reshape(LEVELS + 1, row_count, half_width)
    zeros_field = jnp.zeros((row_count, half_width), jnp.float32)
    earlier = entering(partials[LEVELS], "lat", add_pair, zeros_field)
    own_errors = []
    squares = []
    for level in range(LEVELS):
        mine = owners[level] == lat_position
        error = dec_bias[None, :] + earlier + partials[level] - resid_full
        own_errors.append(jnp.where(mine, error, 0.0))
        squares.append(jnp.where(mine, jnp.sum(error * error), 0.0))
    include = (level_bounds[:, None] > local_ids[None, :]).astype(jnp.float32)
    err_sum = None
    for level in range(LEVELS):
        level_err = broadcast(own_errors[level], "lat", owners[level])
        term = include[level][:, None, None] * level_err[None]
        err_sum = term if err_sum is None else err_sum + term
    err_half = err_sum.astype(jnp.bfloat16)
    partial_adjoint = jnp.einsum(
        "ktd,kcd->tkc", err_half, dict_blocks, preferred_element_type=jnp.float32
    )
    g_act = lax.psum(partial_adjoint.reshape(row_count, lat_count), "wid")
    mask_full = jnp.broadcast_to(hits[:, :, None], (row_count, blocks_here, 128)).reshape(
        row_count, lat_count
    )
    _, pull = jax.vjp(gelu_tanh, pre)
    g_pre = pull(g_act * mask_full)[0].astype(jnp.bfloat16)
    decode_term = jnp.einsum("ktd,tkc->dkc", err_half, act, preferred_element_type=jnp.float32)
    encode_term = lax.dot_general(
        resid, g_pre, (((0,), (0,)), ((), ())), preferred_element_type=jnp.float32
    )
    grad_share = lax.psum_scatter(
        decode_term.reshape(half_width // lax.axis_size("tok") * lax.axis_size("tok"), lat_count)
        + encode_term,
        "tok",
        scatter_dimension=0,
        tiled=True,
    )
    total_sq = lax.psum(jnp.stack(squares), ("lat", "wid", "tok"))
    level_losses = total_sq / (row_count * lax.axis_size("tok") * half_width * lax.axis_size("wid"))
    return (level_losses, grad_share.astype(jnp.bfloat16))


def solution(mesh):
    return jax.shard_map(
        body,
        mesh=mesh,
        in_specs=(P("tok", "wid"), P("lat", "wid"), P("lat"), P("wid"), P("tok", None), P()),
        out_specs=(P(), P(("wid", "tok"), "lat")),
        check_vma=False,
    )
```

profile of v0, /device:TPU:1, one launch (start us, length us, event | category | flops | bytes accessed | tf_op | source)
XLA Modules:
  0.0 1121.9 jit_solution(13684418029557174763)
XLA Ops:
  7.2 1.5 copy-done
  8.8 2.6 fusion.25
  11.4 0.0 all-gather.3.cloned.1.call-start
  11.4 1.5 fusion.23
  12.9 0.8 compare_reduce_fusion
  16.2 0.1 copy.17
  16.4 41.2 %all-reduce.5.cloned.1.call-done = f32[128,512]{1,0:T(8,128)} async-done(((f32[128,512]{1,0:T(8,128)}), f32[128,512]{1,0:T(8,128)}) %all-reduce.5.cloned.1.call-update) | async-done | bytes 262160 | tf_op jit(solution)/shard_map/psum | solution.py:45
  57.6 1.8 multiply_convert_fusion.1
  59.4 1.6 fusion.26
  61.0 2.3 copy-done.1
  63.3 1.1 slice.60
  64.6 512.8 %all-gather.3.cloned.1.call-done = f32[8192,2048]{1,0:T(8,128)} async-done(((f32[128,2048]{1,0:T(8,128)}), f32[8192,2048]{1,0:T(8,128)}) %all-gather.3.cloned.1.call-update) | async-done | bytes 67108880 | tf_op jit(solution)/shard_map/all_gather | solution.py:11
  577.4 0.1 broadcast.226
  577.6 0.7 copy-done.6
  578.2 5.8 select_select_fusion.3
  584.0 0.0 all-reduce.7.cloned.1.call-start
  584.1 0.6 copy-done.5
  584.7 0.1 compare_convert_fusion
  584.7 0.2 copy-done.3
  585.0 0.1 copy.18
  585.1 365.0 %all-reduce.9.cloned.1.call-done = (f32[128,2048]{1,0:T(8,128)}, f32[128,2048]{1,0:T(8,128)}, f32[128,2048]{1,0:T(8,128)}, f32[128,2048]{1,0:T(8,128)}) async-done(((f32[128,2048]{1,0:T(8,128)}, f32[128,2048]{1,0:T(8,128)}, f32[128,2048]{1,0:T(8,128)}, f32[128,2048]{1,0:T(8,128)}), (f32[128,2048]{1,0:T(8,128)}, f32[128,2048]{1,0:T(8,128)}, f32[128,2048]{1,0:T(8,128)}, ...) | async-done | bytes 4194320 | tf_op jit(solution)/shard_map/psum | solution.py:22
  950.1 3.5 fusion.24
  953.6 0.8 copy.19
  954.5 0.0 reduce-scatter.2.cloned.1.call-start
  954.6 5.7 fusion.7
  960.2 39.1 %all-reduce.7.cloned.1.call-done = f32[128,512]{1,0:T(8,128)} async-done(((f32[128,512]{1,0:T(8,128)}), f32[128,512]{1,0:T(8,128)}) %all-reduce.7.cloned.1.call-update) | async-done | bytes 262160 | tf_op jit(solution)/shard_map/psum | solution.py:89
  999.3 5.1 bitcast_add_fusion.1
  1007.1 0.1 pad_maximum_fusion
  1007.1 105.4 %psum.50 = f32[4]{0:T(128)S(1)} all-reduce(f32[4]{0:T(128)S(1)} %pad_maximum_fusion), channel_id=1, replica_groups=mesh['lat'=64,'wid'=2,'tok'=4] {'lat','wid','tok'}, use_global_device_ids=true, to_apply=%region_8.9 | all-reduce | flops 4 | bytes 32 | tf_op jit(solution)/shard_map/psum | solution.py:106
  1112.6 0.5 broadcast_multiply_fusion
  1113.1 1.3 convert_element_type.36
  1114.4 1.0 copy.16
  (29 shorter events, 0.4 us)
Async XLA Ops:
  7.2 1.6 copy-start
  7.2 50.4 %all-reduce.5.cloned.1.call-start = ((), (), s32[]{:S(2)}) async-start(), calls=%async_computation.1 | async-start | bytes 524288 | tf_op jit(solution)/shard_map/psum | solution.py:45
  11.4 566.1 %all-gather.3.cloned.1.call-start = ((), (), s32[]{:S(2)}) async-start(), calls=%async_computation.4 | async-start | bytes 68157440 | tf_op jit(solution)/shard_map/all_gather | solution.py:11
  61.0 2.3 copy-start.1
  64.4 885.7 %all-reduce.9.cloned.1.call-start = ((), (), s32[]{:S(2)}) async-start(), calls=%async_computation.5 | async-start | bytes 8388608 | tf_op jit(solution)/shard_map/psum | solution.py:22
  577.5 0.7 copy-start.6
  584.0 0.7 copy-start.5
  584.0 1.0 copy-start.3
  584.0 415.3 %all-reduce.7.cloned.1.call-start = ((), (), s32[]{:S(2)}) async-start(), calls=%async_computation.2 | async-start | bytes 524288 | tf_op jit(solution)/shard_map/psum | solution.py:89
  954.5 158.6 %reduce-scatter.2.cloned.1.call-start = ((), (), s32[]{:S(2)}) async-start(), calls=%async_computation.3 | async-start | bytes 5242880 | tf_op jit(solution)/shard_map/reduce_scatter | solution.py:99
  954.5 44.8 %copy-start.2 = (bf16[128,2048]{1,0:T(8,128)(2,1)S(1)}, bf16[128,2048]{1,0:T(8,128)(2,1)}, u32[]{:S(2)}) copy-start(bf16[128,2048]{1,0:T(8,128)(2,1)} %param.8) | copy-start | bytes 1572868
  954.5 44.8 %copy-start.4 = (f32[128,512]{1,0:T(8,128)S(1)}, f32[128,512]{1,0:T(8,128)}, u32[]{:S(2)}) copy-start(f32[128,512]{1,0:T(8,128)} %all-reduce.5.cloned.1.call-done) | copy-start | bytes 786436
  954.5 44.8 %copy-start.7 = (f32[512]{0:T(512)S(1)}, f32[512]{0:T(512)}, u32[]{:S(2)}) copy-start(f32[512]{0:T(512)} %param.10) | copy-start | bytes 6148
Sparse Core Ops, SparseCore 0:
  11.5 46.0 all-reduce.4
  64.6 512.8 all-gather.2
  584.2 365.8 all-reduce.8
  954.6 44.6 all-reduce.6
  1004.6 54.7 reduce-scatter.1
where the time goes:
time: 1120 us
  waiting for transfers between devices  958 us (86%)
  blocking collectives  105 us (9%)
  between operations  19.2 us (2%)
  matrix products  18.4 us (2%)
    all_gather x1, waiting for transfers between devices, entering(): gathered = lax.all_gather(part, axis)  513 us
    psum x1, waiting for transfers between devices, broadcast(): return lax.psum(jnp.where(mine, array, jnp.zeros_like(array)), axis)  365 us
    psum x1, blocking collectives, body(): total_sq = lax.psum(jnp.stack(squares), ('lat', 'wid', 'tok'))  105 us
    psum x1, waiting for transfers between devices, body(): pre = lax.psum(partial_pre, 'wid') + enc_bias[None, :]  41.2 us
    psum x1, waiting for transfers between devices, body(): g_act = lax.psum(partial_adjoint.reshape(row_count, lat_count), 'wid')  39.1 us
  transfers between devices with their start and end apart: 5, of which 4 were waited for; matrix products, arithmetic and copies ran while one was open for 1% of the time, Pallas kernels for 0%

commit v1 on v0

v1 whole, which is shorter than its diff:
```python
import functools

import jax
import jax.numpy as jnp
from jax import lax
from jax.experimental import pallas as pl
from jax.experimental.pallas import tpu as pltpu
from jax.sharding import PartitionSpec as P

LEVELS = 4
MESH_ID = pl.DeviceIdType.MESH


def gelu_tanh(value):
    return jax.nn.gelu(value, approximate=True)


def device_on(axis_names, moved):
    return tuple(moved[n] if n in moved else lax.axis_index(n) for n in axis_names)


def pair_sum_kernel(axis_names, x_ref, out_ref, held, send_sem, recv_sem):
    me = lax.axis_index("wid")
    other = device_on(axis_names, {"wid": 1 - me})
    barrier = pltpu.get_barrier_semaphore()
    pl.semaphore_signal(barrier, 1, device_id=other, device_id_type=MESH_ID)
    pl.semaphore_wait(barrier, 1)
    copy = pltpu.make_async_remote_copy(
        src_ref=x_ref, dst_ref=held, send_sem=send_sem, recv_sem=recv_sem,
        device_id=other, device_id_type=MESH_ID,
    )
    copy.start()
    copy.wait()
    out_ref[...] = x_ref[...] + held[...]


def pair_sum(x, axis_names, cid):
    return pl.pallas_call(
        functools.partial(pair_sum_kernel, axis_names),
        out_shape=jax.ShapeDtypeStruct(x.shape, x.dtype),
        in_specs=[pl.BlockSpec(memory_space=pltpu.VMEM)],
        out_specs=pl.BlockSpec(memory_space=pltpu.VMEM),
        scratch_shapes=[
            pltpu.VMEM(x.shape, x.dtype),
            pltpu.SemaphoreType.DMA(()),
            pltpu.SemaphoreType.DMA(()),
        ],
        compiler_params=pltpu.CompilerParams(collective_id=cid, has_side_effects=True),
    )(x)


def lat_sum_kernel(axis_names, ny, nz, x_ref, out_ref, recv1, ybuf, recv2, zbuf, yfull,
                   s1, r1, s2, r2, s3, r3, s4, r4):
    lat = lax.axis_index("lat")
    my_y = lat % ny
    my_z = lat // ny
    rows = x_ref.shape[1]
    cz = rows // nz

    def y_dev(c):
        return device_on(axis_names, {"lat": my_z * ny + c})

    def z_dev(c):
        return device_on(axis_names, {"lat": c * ny + my_y})

    def zrows(c):
        return pl.ds(pl.multiple_of(c * cz, cz), cz)

    barrier = pltpu.get_barrier_semaphore()
    for d in range(1, ny):
        pl.semaphore_signal(barrier, 1, device_id=y_dev((my_y + d) % ny), device_id_type=MESH_ID)
    for d in range(1, nz):
        pl.semaphore_signal(barrier, 1, device_id=z_dev((my_z + d) % nz), device_id_type=MESH_ID)
    pl.semaphore_wait(barrier, (ny - 1) + (nz - 1))

    sends = []
    for d in range(1, ny):
        c = (my_y + d) % ny
        cp = pltpu.make_async_remote_copy(
            src_ref=x_ref.at[c], dst_ref=recv1.at[my_y], send_sem=s1.at[c], recv_sem=r1.at[my_y],
            device_id=y_dev(c), device_id_type=MESH_ID,
        )
        cp.start()
        sends.append(cp)
    recv1[my_y] = x_ref[my_y]
    for d in range(1, ny):
        src = (my_y + ny - d) % ny
        pltpu.make_async_remote_copy(
            src_ref=x_ref.at[src], dst_ref=recv1.at[src], send_sem=s1.at[src], recv_sem=r1.at[src],
            device_id=y_dev(src), device_id_type=MESH_ID,
        ).wait_recv()
    total = recv1[0]
    for s in range(1, ny):
        total = total + recv1[s]
    ybuf[...] = total
    for cp in sends:
        cp.wait_send()

    sends = []
    for d in range(1, nz):
        c = (my_z + d) % nz
        cp = pltpu.make_async_remote_copy(
            src_ref=ybuf.at[zrows(c)], dst_ref=recv2.at[my_z], send_sem=s2.at[c], recv_sem=r2.at[my_z],
            device_id=z_dev(c), device_id_type=MESH_ID,
        )
        cp.start()
        sends.append(cp)
    recv2[my_z] = ybuf[zrows(my_z)]
    for d in range(1, nz):
        src = (my_z + nz - d) % nz
        pltpu.make_async_remote_copy(
            src_ref=ybuf.at[zrows(src)], dst_ref=recv2.at[src], send_sem=s2.at[src], recv_sem=r2.at[src],
            device_id=z_dev(src), device_id_type=MESH_ID,
        ).wait_recv()
    total = recv2[0]
    for s in range(1, nz):
        total = total + recv2[s]
    zbuf[...] = total
    for cp in sends:
        cp.wait_send()

    sends = []
    for d in range(1, nz):
        c = (my_z + d) % nz
        cp = pltpu.make_async_remote_copy(
            src_ref=zbuf, dst_ref=yfull.at[zrows(my_z)], send_sem=s3.at[c], recv_sem=r3.at[my_z],
            device_id=z_dev(c), device_id_type=MESH_ID,
        )
        cp.start()
        sends.append(cp)
    yfull[zrows(my_z)] = zbuf[...]
    for d in range(1, nz):
        src = (my_z + nz - d) % nz
        pltpu.make_async_remote_copy(
            src_ref=zbuf, dst_ref=yfull.at[zrows(src)], send_sem=s3.at[src], recv_sem=r3.at[src],
            device_id=z_dev(src), device_id_type=MESH_ID,
        ).wait_recv()
    for cp in sends:
        cp.wait_send()

    sends = []
    for d in range(1, ny):
        c = (my_y + d) % ny
        cp = pltpu.make_async_remote_copy(
            src_ref=yfull, dst_ref=out_ref.at[my_y], send_sem=s4.at[c], recv_sem=r4.at[my_y],
            device_id=y_dev(c), device_id_type=MESH_ID,
        )
        cp.start()
        sends.append(cp)
    out_ref[my_y] = yfull[...]
    for d in range(1, ny):
        src = (my_y + ny - d) % ny
        pltpu.make_async_remote_copy(
            src_ref=yfull, dst_ref=out_ref.at[src], send_sem=s4.at[src], recv_sem=r4.at[src],
            device_id=y_dev(src), device_id_type=MESH_ID,
        ).wait_recv()
    for cp in sends:
        cp.wait_send()


def lat_sum(x, axis_names, n_lat, cid):
    ny = 4 if n_lat % 4 == 0 else 1
    nz = n_lat // ny
    chunks, rows, width = x.shape
    assert chunks == ny and rows % (8 * nz) == 0
    cz = rows // nz
    f32 = jnp.float32
    return pl.pallas_call(
        functools.partial(lat_sum_kernel, axis_names, ny, nz),
        out_shape=jax.ShapeDtypeStruct(x.shape, x.dtype),
        in_specs=[pl.BlockSpec(memory_space=pltpu.VMEM)],
        out_specs=pl.BlockSpec(memory_space=pltpu.VMEM),
        scratch_shapes=[
            pltpu.VMEM((ny, rows, width), f32),
            pltpu.VMEM((rows, width), f32),
            pltpu.VMEM((nz, cz, width), f32),
            pltpu.VMEM((cz, width), f32),
            pltpu.VMEM((rows, width), f32),
            pltpu.SemaphoreType.DMA((ny,)),
            pltpu.SemaphoreType.DMA((ny,)),
            pltpu.SemaphoreType.DMA((nz,)),
            pltpu.SemaphoreType.DMA((nz,)),
            pltpu.SemaphoreType.DMA((nz,)),
            pltpu.SemaphoreType.DMA((nz,)),
            pltpu.SemaphoreType.DMA((ny,)),
            pltpu.SemaphoreType.DMA((ny,)),
        ],
        compiler_params=pltpu.CompilerParams(
            collective_id=cid, has_side_effects=True, vmem_limit_bytes=48 * 1024 * 1024
        ),
    )(x)


def body(axis_names, n_lat, resid, dictionary, enc_bias, dec_bias, active_blocks, level_bounds):
    row_count, half_width = resid.shape
    lat_count = dictionary.shape[0]
    blocks_here = lat_count // 128
    lat_position = lax.axis_index("lat")
    first_block = lat_position * blocks_here
    local_ids = first_block + jnp.arange(blocks_here, dtype=jnp.int32)
    resid_full = resid.astype(jnp.float32)
    dict_blocks = dictionary.reshape(blocks_here, 128, half_width)

    partial_pre = lax.dot_general(
        resid, dictionary, (((1,), (1,)), ((), ())), preferred_element_type=jnp.float32
    )
    pre = pair_sum(partial_pre, axis_names, 1) + enc_bias[None, :]
    hits = jnp.any(active_blocks[:, :, None] == local_ids[None, None, :], axis=1).astype(
        jnp.float32
    )
    act = (gelu_tanh(pre).reshape(row_count, blocks_here, 128) * hits[:, :, None]).astype(
        jnp.bfloat16
    )
    act_flat = act.reshape(row_count, lat_count)

    latent_block = first_block + jnp.arange(lat_count, dtype=jnp.int32) // 128
    keep = latent_block[None, :] < level_bounds[:, None]
    act_stack = jnp.where(keep[:, None, :], act_flat[None], jnp.zeros((), jnp.bfloat16))
    contrib = jnp.dot(
        act_stack.reshape(LEVELS * row_count, lat_count),
        dictionary,
        preferred_element_type=jnp.float32,
    ).reshape(LEVELS, row_count, half_width)
    levels = lat_sum(contrib, axis_names, n_lat, 0)

    errors = dec_bias[None, None, :] + levels - resid_full[None]
    squares = jnp.sum(errors * errors, axis=(1, 2))
    total_sq = lax.psum(squares, ("wid", "tok"))
    level_losses = total_sq / (row_count * lax.axis_size("tok") * half_width * lax.axis_size("wid"))
    cum_err = jnp.cumsum(errors[::-1], axis=0)[::-1].astype(jnp.bfloat16)

    level_of = jnp.sum((level_bounds[None, :] <= local_ids[:, None]).astype(jnp.int32), axis=1)
    err_half = jnp.take(cum_err, level_of, axis=0)
    partial_adjoint = jnp.einsum(
        "ktd,kcd->tkc", err_half, dict_blocks, preferred_element_type=jnp.float32
    )
    g_act = pair_sum(partial_adjoint.reshape(row_count, lat_count), axis_names, 2)
    mask_full = jnp.broadcast_to(hits[:, :, None], (row_count, blocks_here, 128)).reshape(
        row_count, lat_count
    )
    _, pull = jax.vjp(gelu_tanh, pre)
    g_pre = pull(g_act * mask_full)[0].astype(jnp.bfloat16)
    decode_term = jnp.einsum("ktd,tkc->dkc", err_half, act, preferred_element_type=jnp.float32)
    encode_term = lax.dot_general(
        resid, g_pre, (((0,), (0,)), ((), ())), preferred_element_type=jnp.float32
    )
    grad_share = lax.psum_scatter(
        decode_term.reshape(half_width, lat_count) + encode_term,
        "tok",
        scatter_dimension=0,
        tiled=True,
    )
    return (level_losses, grad_share.astype(jnp.bfloat16))


def solution(mesh):
    axis_names = tuple(mesh.axis_names)
    n_lat = mesh.shape["lat"]
    return jax.shard_map(
        functools.partial(body, axis_names, n_lat),
        mesh=mesh,
        in_specs=(P("tok", "wid"), P("lat", "wid"), P("lat"), P("wid"), P("tok", None), P()),
        out_specs=(P(), P(("wid", "tok"), "lat")),
        check_vma=False,
    )
```

time: 1120 us -> 323 us (0.29)
  waiting for transfers between devices: 958 us -> 36.1 us
  Pallas kernels: 0 us -> 215 us
  blocking collectives: 105 us -> 15 us
    all_gather x1 -> x0, waiting for transfers between devices: 513 us -> none  [entering(): gathered = lax.all_gather(part, axis)]
    psum x3 -> x0, waiting for transfers between devices: 445 us -> none  [the longest x1 365 us: broadcast(): return lax.psum(jnp.where(mine, array, jnp.zeros_like(array)), axis)]
    pallas_call x0 -> x3, Pallas kernels: none -> 215 us  [the longest x1 199 us: lat_sum(): pl.pallas_call(functools.partial(lat_sum_kernel, axis_names, ny, nz), out...]
    psum x1, blocking collectives: 105 us -> 15 us  [body(): total_sq = lax.psum(squares, ('wid', 'tok'))]
    reduce_scatter x1, waiting for transfers between devices: 0.01 us -> 36.1 us  [body(): lax.psum_scatter(decode_term.reshape(half_width, lat_count) + encode_term...]
  transfers between devices with their start and end apart: 5 -> 1, of which waited for: 4 -> 1; matrix products, arithmetic and copies ran while one was open for 1% -> 0% of each run, Pallas kernels for 0% -> 0%
where the time goes in v1:
time: 323 us; the launch traced here: 322 us
  Pallas kernels  215 us (67%)
  waiting for transfers between devices  36.1 us (11%)
  matrix products  15.1 us (5%)
  blocking collectives  15 us (5%)
  between operations  14.2 us (4%)
  local copies, waits for them, and re-layouts  13.6 us (4%)
  other arithmetic  13.4 us (4%)
    pallas_call x1, Pallas kernels, lat_sum(): pl.pallas_call(functools.partial(lat_sum_kernel, axis_names, ny, nz), out...  199 us
    reduce_scatter x1, waiting for transfers between devices, body(): lax.psum_scatter(decode_term.reshape(half_width, lat_count) + encode_term...  36.1 us
    pallas_call x2, Pallas kernels, pair_sum(): pl.pallas_call(functools.partial(pair_sum_kernel, axis_names), out_shape=...  15.7 us
    psum x1, blocking collectives, body(): total_sq = lax.psum(squares, ('wid', 'tok'))  15 us
    rev x2, local copies, waits for them, and re-layouts, body(): cum_err = jnp.cumsum(errors[::-1], axis=0)[::-1].astype(jnp.bfloat16)  7.8 us
  transfers between devices with their start and end apart: 1, of which 1 were waited for; matrix products, arithmetic and copies ran while one was open for 0% of the time, Pallas kernels for 0%

profile of v1, /device:TPU:1, one launch (start us, length us, event | category | flops | bytes accessed | tf_op | source)
XLA Modules:
  0.0 322.4 jit_solution(8654518512789661369)
XLA Ops:
  7.2 0.0 copy-start
  7.2 0.0 copy-start.2
  7.2 0.0 reduce-scatter.2.cloned.1.call-start
  7.3 1.0 convert_reduce_fusion
  8.3 0.8 compare_reduce_fusion
  9.1 0.1 copy.17
  9.2 2.1 convert_element_type.31
  11.3 0.0 copy-done.2
  11.4 1.5 fusion.39.x_ref
  12.9 10.4 %shard_map.77 = f32[128,512]{1,0:T(8,128)} custom-call(f32[128,512]{1,0:T(8,128)} %fusion.39.x_ref), custom_call_target="tpu_custom_call" | custom-call | tf_op jit(solution)/shard_map/pallas_call | solution.py:38
  23.3 0.0 copy-done.7
  23.3 0.1 broadcast_compare_fusion
  23.4 1.1 multiply_convert_fusion.1
  24.5 3.2 fusion.x_ref
  27.7 199.3 %shard_map.78 = f32[4,128,2048]{2,1,0:T(8,128)S(1)} custom-call(f32[4,128,2048]{2,1,0:T(8,128)} %fusion.x_ref), custom_call_target="tpu_custom_call" | custom-call | tf_op jit(solution)/shard_map/pallas_call | solution.py:168
  227.0 2.8 multiply_reduce_fusion
  229.8 4.6 %rev.6 = f32[4,128,2048]{2,1,0:T(8,128)} reverse(f32[4,128,2048]{2,1,0:T(8,128)} %get-tuple-element.7), dimensions={0} | reverse | bytes 8388608 | tf_op jit(solution)/shard_map/rev | solution.py:230
  234.4 3.7 %fusion.38 = bf16[4,128,2048]{2,1,0:T(8,128)(2,1)} fusion(f32[4,128,2048]{2,1,0:T(8,128)} %rev.6), kind=kOutput, calls=%fused_computation.61 | output fusion | flops 3145728 | bytes 6291456 | tf_op jit(solution)/shard_map/jit(cumsum)/reduce_window_sum | solution.py:230
  238.1 3.2 rev.9
  241.3 0.1 copy.18
  241.5 3.6 %gather_fusion = bf16[4,128,2048]{2,1,0:T(8,128)(2,1)} fusion(bf16[4,128,2048]{2,1,0:T(8,128)(2,1)} %rev.9, s32[1024]{0:T(1024)S(1)} %pad_clamp_fusion), kind=kCustom, calls=%fused_computation | custom fusion | bytes 4194320 | tf_op jit(solution)/shard_map/jit(_take)/gather | solution.py:233
  245.1 4.4 %fusion.3 = f32[4,128,2048]{2,1,0:T(8,128)} fusion(bf16[4,128,2048]{2,1,0:T(8,128)(2,1)} %gather_fusion, pred[4]{0:T(512)(128)(4,1)S(1)} %compare_and_fusion, f32[128,4,128]{0,2,1:T(8,128)S(1)} %bitcast.25, f32[128,4]{0,1:T(4,128)S(1)} %convert_element_type.29), kind=kOutput, calls=%fused_computation.9 | convolution fusion | flops 269615104 | bytes 6555652 | tf_op jit(solution)/shard_map/ktd,tkc->dkc/dot_general | solution.py:243
  249.5 0.8 fusion.2
  250.3 0.8 copy.19.x_ref
  251.2 5.2 %shard_map.79 = f32[128,512]{1,0:T(8,128)} custom-call(f32[128,512]{1,0:T(8,128)} %copy.19.x_ref), custom_call_target="tpu_custom_call" | custom-call | tf_op jit(solution)/shard_map/pallas_call | solution.py:38
  256.4 5.1 %bitcast_add_fusion = f32[2048,512]{0,1:T(8,128)} fusion(f32[4,128,2048]{2,1,0:T(8,128)} %fusion.3, bf16[128,2048]{1,0:T(8,128)(2,1)S(1)} %copy-done.2, f32[128,512]{1,0:T(8,128)} %shard_map.79, f32[128,512]{1,0:T(8,128)S(1)} %copy.17, f32[128,512]{1,0:T(8,128)S(1)} %copy-done.4, f32[512]{0:T(512)S(1)} %copy-done.6), kind=kOutput, calls=%fused_computation.1 | convolution fusion | flops 270925824 | bytes 9701376 | tf_op jit(solution)/shard_map/dot_general | solution.py:244
  261.6 0.0 reduce-scatter.2.cloned.1.call-update
  261.6 15.0 %psum.7 = f32[4]{0:T(128)S(1)} all-reduce(f32[4]{0:T(128)S(1)} %get-tuple-element.6), channel_id=1, replica_groups=mesh['lat'=64,'wid'=2,'tok'=4] {'wid','tok'}, use_global_device_ids=true, to_apply=%region_2.3 | all-reduce | flops 4 | bytes 32 | tf_op jit(solution)/shard_map/psum | solution.py:228
  276.6 0.5 broadcast_multiply_fusion
  277.1 36.1 %reduce-scatter.2.cloned.1.call-done = f32[512,512]{0,1:T(8,128)} async-done(((f32[2048,512]{0,1:T(8,128)}), f32[512,512]{0,1:T(8,128)}) %reduce-scatter.2.cloned.1.call-update) | async-done | bytes 1048592 | tf_op jit(solution)/shard_map/reduce_scatter | solution.py:247
  313.3 1.3 convert_element_type.36
  314.6 1.0 copy.16
  (19 shorter events, 0.1 us)
Async XLA Ops:
  7.2 4.2 %copy-start = (bf16[512,2048]{1,0:T(8,128)(2,1)S(1)}, bf16[512,2048]{1,0:T(8,128)(2,1)}, u32[]{:S(2)}) copy-start(bf16[512,2048]{1,0:T(8,128)(2,1)} %param.7) | copy-start | bytes 6291460
  7.2 4.2 %copy-start.2 = (bf16[128,2048]{1,0:T(8,128)(2,1)S(1)}, bf16[128,2048]{1,0:T(8,128)(2,1)}, u32[]{:S(2)}) copy-start(bf16[128,2048]{1,0:T(8,128)(2,1)} %param.6) | copy-start | bytes 1572868
  7.2 306.1 %reduce-scatter.2.cloned.1.call-start = ((), (), s32[]{:S(2)}) async-start(), calls=%async_computation.1 | async-start | bytes 5242880 | tf_op jit(solution)/shard_map/reduce_scatter | solution.py:247
  11.3 12.0 %copy-start.7 = (s32[4]{0:T(128)S(1)}, s32[4]{0:T(128)}, u32[]{:S(2)}) copy-start(s32[4]{0:T(128)} %param.11) | copy-start | bytes 52
  11.4 12.1 %copy-start.6 = (f32[512]{0:T(512)S(1)}, f32[512]{0:T(512)}, u32[]{:S(2)}) copy-start(f32[512]{0:T(512)} %param.8) | copy-start | bytes 6148
  27.7 199.3 %copy-start.3 = (f32[128,2048]{1,0:T(8,128)S(1)}, f32[128,2048]{1,0:T(8,128)}, u32[]{:S(2)}) copy-start(f32[128,2048]{1,0:T(8,128)} %convert_element_type.31) | copy-start | bytes 3145732
  27.7 199.3 %copy-start.5 = (f32[2048]{0:T(1024)S(1)}, f32[2048]{0:T(1024)}, u32[]{:S(2)}) copy-start(f32[2048]{0:T(1024)} %param.9) | copy-start | bytes 24580
  245.1 4.4 %copy-start.1 = (bf16[4,128,2048]{2,1,0:T(8,128)(2,1)S(1)}, bf16[4,128,2048]{2,1,0:T(8,128)(2,1)}, u32[]{:S(2)}) copy-start(bf16[4,128,2048]{2,1,0:T(8,128)(2,1)} %gather_fusion) | copy-start | bytes 6291460
  249.5 6.9 %copy-start.4 = (f32[128,512]{1,0:T(8,128)S(1)}, f32[128,512]{1,0:T(8,128)}, u32[]{:S(2)}) copy-start(f32[128,512]{1,0:T(8,128)} %shard_map.77) | copy-start | bytes 786436
Sparse Core Ops, SparseCore 0:
  261.7 51.4 reduce-scatter.1

commit v2 on v0

v2 whole, which is shorter than its diff:
```python
import functools

import jax
import jax.numpy as jnp
from jax import lax
from jax.experimental import pallas as pl
from jax.experimental.pallas import tpu as pltpu
from jax.sharding import PartitionSpec as P

LEVELS = 4
MESH_ID = pl.DeviceIdType.MESH


def gelu_tanh(value):
    return jax.nn.gelu(value, approximate=True)


def device_on(axis_names, moved):
    return tuple(moved[n] if n in moved else lax.axis_index(n) for n in axis_names)


def remote(src, dst, send_sem, recv_sem, device):
    return pltpu.make_async_remote_copy(
        src_ref=src, dst_ref=dst, send_sem=send_sem, recv_sem=recv_sem,
        device_id=device, device_id_type=MESH_ID,
    )


def gather_phase(n, pos, dev_of, src_of, slot_of, send_sems, recv_sems):
    sends = []
    for d in range(1, n):
        c = (pos + d) % n
        cp = remote(src_of(c), slot_of(pos), send_sems.at[c], recv_sems.at[pos], dev_of(c))
        cp.start()
        sends.append(cp)
    slot_of(pos)[...] = src_of(pos)[...]
    for d in range(1, n):
        s = (pos + n - d) % n
        remote(src_of(s), slot_of(s), send_sems.at[s], recv_sems.at[s], dev_of(s)).wait_recv()
    return sends


def axis_sum_kernel(axis_names, axis, n, x_ref, out_ref, slots, send_sem, recv_sem):
    me = lax.axis_index(axis)

    def dev_of(c):
        return device_on(axis_names, {axis: c})

    barrier = pltpu.get_barrier_semaphore()
    for d in range(1, n):
        pl.semaphore_signal(barrier, 1, device_id=dev_of((me + d) % n), device_id_type=MESH_ID)
    pl.semaphore_wait(barrier, n - 1)
    sends = gather_phase(n, me, dev_of, lambda c: x_ref, lambda c: slots.at[c], send_sem, recv_sem)
    total = slots[0]
    for s in range(1, n):
        total = total + slots[s]
    out_ref[...] = total
    for cp in sends:
        cp.wait_send()


def axis_sum(x, axis_names, axis, n, cid):
    return pl.pallas_call(
        functools.partial(axis_sum_kernel, axis_names, axis, n),
        out_shape=jax.ShapeDtypeStruct(x.shape, x.dtype),
        in_specs=[pl.BlockSpec(memory_space=pltpu.VMEM)],
        out_specs=pl.BlockSpec(memory_space=pltpu.VMEM),
        scratch_shapes=[
            pltpu.VMEM((n,) + x.shape, x.dtype),
            pltpu.SemaphoreType.DMA((n,)),
            pltpu.SemaphoreType.DMA((n,)),
        ],
        compiler_params=pltpu.CompilerParams(collective_id=cid, has_side_effects=True),
    )(x)


def lat_sum_kernel(axis_names, ny, nlo, nhi, x_ref, out_ref, recv1, recv2, recv3, part3, part2, part1,
                   ag2, ag1, sems):
    lat = lax.axis_index("lat")
    my_y = lat % ny
    my_z = lat // ny
    my_lo = my_z % nlo
    my_hi = my_z // nlo
    rows = x_ref.shape[1]
    c2 = rows // nlo
    c3 = c2 // nhi

    def y_dev(c):
        return device_on(axis_names, {"lat": my_z * ny + c})

    def lo_dev(c):
        return device_on(axis_names, {"lat": (my_hi * nlo + c) * ny + my_y})

    def hi_dev(c):
        return device_on(axis_names, {"lat": (c * nlo + my_lo) * ny + my_y})

    def rows_of(c, size):
        return pl.ds(pl.multiple_of(c * size, size), size)

    barrier = pltpu.get_barrier_semaphore()
    for n, pos, dev_of in ((ny, my_y, y_dev), (nlo, my_lo, lo_dev), (nhi, my_hi, hi_dev)):
        for d in range(1, n):
            pl.semaphore_signal(barrier, 1, device_id=dev_of((pos + d) % n), device_id_type=MESH_ID)
    pl.semaphore_wait(barrier, (ny - 1) + (nlo - 1) + (nhi - 1))

    def summed(slots, n):
        total = slots[0]
        for s in range(1, n):
            total = total + slots[s]
        return total

    sends = gather_phase(ny, my_y, y_dev, lambda c: x_ref.at[c], lambda c: recv1.at[c],
                         sems.at[0, 0], sems.at[0, 1])
    part1[...] = summed(recv1, ny)
    for cp in sends:
        cp.wait_send()
    sends = gather_phase(nlo, my_lo, lo_dev, lambda c: part1.at[rows_of(c, c2)], lambda c: recv2.at[c],
                         sems.at[1, 0], sems.at[1, 1])
    part2[...] = summed(recv2, nlo)
    for cp in sends:
        cp.wait_send()
    sends = gather_phase(nhi, my_hi, hi_dev, lambda c: part2.at[rows_of(c, c3)], lambda c: recv3.at[c],
                         sems.at[2, 0], sems.at[2, 1])
    part3[...] = summed(recv3, nhi)
    for cp in sends:
        cp.wait_send()
    sends = gather_phase(nhi, my_hi, hi_dev, lambda c: part3, lambda c: ag2.at[rows_of(c, c3)],
                         sems.at[3, 0], sems.at[3, 1])
    for cp in sends:
        cp.wait_send()
    sends = gather_phase(nlo, my_lo, lo_dev, lambda c: ag2, lambda c: ag1.at[rows_of(c, c2)],
                         sems.at[4, 0], sems.at[4, 1])
    for cp in sends:
        cp.wait_send()
    sends = gather_phase(ny, my_y, y_dev, lambda c: ag1, lambda c: out_ref.at[c],
                         sems.at[5, 0], sems.at[5, 1])
    for cp in sends:
        cp.wait_send()


def lat_sum(x, axis_names, n_lat, cid):
    ny = 4 if n_lat % 4 == 0 else 1
    nz = n_lat // ny
    nlo = 4 if nz % 4 == 0 else nz
    nhi = nz // nlo
    chunks, rows, width = x.shape
    assert chunks == ny and rows % (8 * nz) == 0
    c2 = rows // nlo
    c3 = c2 // nhi
    f32 = jnp.float32
    most = max(ny, nlo, nhi)
    return pl.pallas_call(
        functools.partial(lat_sum_kernel, axis_names, ny, nlo, nhi),
        out_shape=jax.ShapeDtypeStruct(x.shape, x.dtype),
        in_specs=[pl.BlockSpec(memory_space=pltpu.VMEM)],
        out_specs=pl.BlockSpec(memory_space=pltpu.VMEM),
        scratch_shapes=[
            pltpu.VMEM((ny, rows, width), f32),
            pltpu.VMEM((nlo, c2, width), f32),
            pltpu.VMEM((nhi, c3, width), f32),
            pltpu.VMEM((c3, width), f32),
            pltpu.VMEM((c2, width), f32),
            pltpu.VMEM((rows, width), f32),
            pltpu.VMEM((c2, width), f32),
            pltpu.VMEM((rows, width), f32),
            pltpu.SemaphoreType.DMA((6, 2, most)),
        ],
        compiler_params=pltpu.CompilerParams(
            collective_id=cid, has_side_effects=True, vmem_limit_bytes=48 * 1024 * 1024
        ),
    )(x)


def body(axis_names, n_lat, resid, dictionary, enc_bias, dec_bias, active_blocks, level_bounds):
    row_count, half_width = resid.shape
    lat_count = dictionary.shape[0]
    blocks_here = lat_count // 128
    lat_position = lax.axis_index("lat")
    first_block = lat_position * blocks_here
    local_ids = first_block + jnp.arange(blocks_here, dtype=jnp.int32)
    resid_full = resid.astype(jnp.float32)
    dict_blocks = dictionary.reshape(blocks_here, 128, half_width)

    partial_pre = lax.dot_general(
        resid, dictionary, (((1,), (1,)), ((), ())), preferred_element_type=jnp.float32
    )
    pre = axis_sum(partial_pre, axis_names, "wid", 2, 1) + enc_bias[None, :]
    hits = jnp.any(active_blocks[:, :, None] == local_ids[None, None, :], axis=1).astype(
        jnp.float32
    )
    act = (gelu_tanh(pre).reshape(row_count, blocks_here, 128) * hits[:, :, None]).astype(
        jnp.bfloat16
    )
    act_flat = act.reshape(row_count, lat_count)

    latent_block = first_block + jnp.arange(lat_count, dtype=jnp.int32) // 128
    keep = latent_block[None, :] < level_bounds[:, None]
    act_stack = jnp.where(keep[:, None, :], act_flat[None], jnp.zeros((), jnp.bfloat16))
    contrib = jnp.dot(
        act_stack.reshape(LEVELS * row_count, lat_count),
        dictionary,
        preferred_element_type=jnp.float32,
    ).reshape(LEVELS, row_count, half_width)
    levels = lat_sum(contrib, axis_names, n_lat, 0)

    errors = dec_bias[None, None, :] + levels - resid_full[None]
    squares = jnp.sum(errors * errors, axis=(1, 2))
    running = errors[LEVELS - 1]
    cum_list = [running]
    for level in range(LEVELS - 2, -1, -1):
        running = running + errors[level]
        cum_list.append(running)
    cum_err = jnp.stack(cum_list[::-1]).astype(jnp.bfloat16)

    level_of = jnp.sum((level_bounds[None, :] <= local_ids[:, None]).astype(jnp.int32), axis=1)
    err_half = jnp.take(cum_err, level_of, axis=0)
    partial_adjoint = jnp.einsum(
        "ktd,kcd->tkc", err_half, dict_blocks, preferred_element_type=jnp.float32
    )
    loss_rows = jnp.zeros((8, lat_count), jnp.float32).at[0, :LEVELS].set(squares)
    adjoint_rows = jnp.concatenate([partial_adjoint.reshape(row_count, lat_count), loss_rows], axis=0)
    summed_rows = axis_sum(adjoint_rows, axis_names, "wid", 2, 2)
    g_act = summed_rows[:row_count]
    loss_tile = jnp.zeros((8, 128), jnp.float32).at[0, :LEVELS].set(summed_rows[row_count, :LEVELS])
    total_sq = axis_sum(loss_tile, axis_names, "tok", lax.axis_size("tok"), 3)[0, :LEVELS]
    level_losses = total_sq / (row_count * lax.axis_size("tok") * half_width * lax.axis_size("wid"))
    mask_full = jnp.broadcast_to(hits[:, :, None], (row_count, blocks_here, 128)).reshape(
        row_count, lat_count
    )
    _, pull = jax.vjp(gelu_tanh, pre)
    g_pre = pull(g_act * mask_full)[0].astype(jnp.bfloat16)
    decode_term = jnp.einsum("ktd,tkc->dkc", err_half, act, preferred_element_type=jnp.float32)
    encode_term = lax.dot_general(
        resid, g_pre, (((0,), (0,)), ((), ())), preferred_element_type=jnp.float32
    )
    grad_share = lax.psum_scatter(
        decode_term.reshape(half_width, lat_count) + encode_term,
        "tok",
        scatter_dimension=0,
        tiled=True,
    )
    return (level_losses, grad_share.astype(jnp.bfloat16))


def solution(mesh):
    axis_names = tuple(mesh.axis_names)
    n_lat = mesh.shape["lat"]
    return jax.shard_map(
        functools.partial(body, axis_names, n_lat),
        mesh=mesh,
        in_specs=(P("tok", "wid"), P("lat", "wid"), P("lat"), P("wid"), P("tok", None), P()),
        out_specs=(P(), P(("wid", "tok"), "lat")),
        check_vma=False,
    )
```

time: 1120 us -> 298 us (0.27)
  waiting for transfers between devices: 958 us -> 46.5 us
  Pallas kernels: 0 us -> 198 us
  blocking collectives: 105 us -> 0 us
    all_gather x1 -> x0, waiting for transfers between devices: 513 us -> none  [entering(): gathered = lax.all_gather(part, axis)]
    psum x3 -> x0, waiting for transfers between devices: 445 us -> none  [the longest x1 365 us: broadcast(): return lax.psum(jnp.where(mine, array, jnp.zeros_like(array)), axis)]
    pallas_call x0 -> x4, Pallas kernels: none -> 198 us  [the longest x1 177 us: lat_sum(): pl.pallas_call(functools.partial(lat_sum_kernel, axis_names, ny, nlo, nhi...]
    psum x1 -> x0, blocking collectives: 105 us -> none  [body(): total_sq = lax.psum(jnp.stack(squares), ('lat', 'wid', 'tok'))]
    reduce_scatter x1, waiting for transfers between devices: 0.01 us -> 46.5 us  [body(): lax.psum_scatter(decode_term.reshape(half_width, lat_count) + encode_term...]
  transfers between devices with their start and end apart: 5 -> 1, of which waited for: 4 -> 1; matrix products, arithmetic and copies ran while one was open for 1% -> 1% of each run, Pallas kernels for 0% -> 2%
where the time goes in v2:
time: 298 us
  Pallas kernels  198 us (66%)
  waiting for transfers between devices  46.5 us (16%)
  matrix products  15.9 us (5%)
  between operations  14.2 us (5%)
  other arithmetic  13.8 us (5%)
  local copies, waits for them, and re-layouts  9.01 us (3%)
    pallas_call x1, Pallas kernels, lat_sum(): pl.pallas_call(functools.partial(lat_sum_kernel, axis_names, ny, nlo, nhi...  177 us
    reduce_scatter x1, waiting for transfers between devices, body(): lax.psum_scatter(decode_term.reshape(half_width, lat_count) + encode_term...  46.5 us
    pallas_call x3, Pallas kernels, axis_sum(): pl.pallas_call(functools.partial(axis_sum_kernel, axis_names, axis, n), o...  21.9 us
  transfers between devices with their start and end apart: 1, of which 1 were waited for; matrix products, arithmetic and copies ran while one was open for 1% of the time, Pallas kernels for 2%

profile of v2, /device:TPU:1, one launch (start us, length us, event | category | flops | bytes accessed | tf_op | source)
XLA Modules:
  0.0 297.8 jit_solution(15499145218383075950)
XLA Ops:
  7.2 0.0 copy-start
  7.2 0.0 reduce-scatter.2.cloned.1.call-start
  7.3 0.9 compare_reduce_fusion
  8.2 0.1 copy.17
  8.4 2.1 convert_element_type.30
  10.5 1.5 fusion.41.x_ref
  12.0 10.4 %shard_map.77 = f32[128,512]{1,0:T(8,128)} custom-call(f32[128,512]{1,0:T(8,128)} %fusion.41.x_ref), custom_call_target="tpu_custom_call" | custom-call | tf_op jit(solution)/shard_map/pallas_call | solution.py:63
  22.5 0.1 broadcast_compare_fusion
  22.6 1.7 multiply_convert_fusion.1
  24.3 3.2 %fusion.x_ref = f32[4,128,2048]{2,1,0:T(8,128)} fusion(bf16[512,2048]{1,0:T(8,128)(2,1)S(1)} %copy-done, pred[4,512]{1,0:T(4,128)(4,1)S(1)} %broadcast_compare_fusion, bf16[128,512]{1,0:T(8,128)(2,1)S(1)} %get-tuple-element.32), kind=kOutput, calls=%fused_computation.5 | convolution fusion | flops 1074003968 | bytes 6424576 | tf_op jit(solution)/shard_map/dot_general | solution.py:199
  27.5 176.5 %shard_map.78 = f32[4,128,2048]{2,1,0:T(8,128)S(1)} custom-call(f32[4,128,2048]{2,1,0:T(8,128)} %fusion.x_ref), custom_call_target="tpu_custom_call" | custom-call | tf_op jit(solution)/shard_map/pallas_call | solution.py:152
  204.1 1.1 multiply_reduce_fusion
  205.2 1.5 fusion.2
  206.7 0.1 slice.92
  206.7 0.2 convert_reduce_fusion
  206.9 1.8 copy.19
  208.7 2.9 pad_maximum_fusion
  211.7 3.6 %gather_fusion = bf16[4,128,2048]{2,1,0:T(8,128)(2,1)} fusion(bf16[4,128,2048]{2,1,0:T(8,128)(2,1)} %pad_maximum_fusion, s32[1024]{0:T(1024)S(1)} %pad_clamp_fusion), kind=kCustom, calls=%fused_computation | custom fusion | bytes 4194320 | tf_op jit(solution)/shard_map/jit(_take)/gather | solution.py:216
  215.3 4.5 %fusion.3 = f32[4,128,2048]{2,1,0:T(8,128)} fusion(bf16[4,128,2048]{2,1,0:T(8,128)(2,1)} %gather_fusion, pred[4]{0:T(512)(128)(4,1)S(1)} %compare_and_fusion, f32[128,4,128]{0,2,1:T(8,128)S(1)} %bitcast.27, f32[128,4]{0,1:T(4,128)S(1)} %convert_element_type.28), kind=kOutput, calls=%fused_computation.13 | convolution fusion | flops 269615104 | bytes 6555652 | tf_op jit(solution)/shard_map/ktd,tkc->dkc/dot_general | solution.py:232
  219.8 1.5 fusion.4
  221.3 1.1 copy.18
  222.4 0.7 select_maximum_fusion.x_ref
  223.1 4.7 %shard_map.79 = f32[136,512]{1,0:T(8,128)} custom-call(f32[136,512]{1,0:T(8,128)} %select_maximum_fusion.x_ref), custom_call_target="tpu_custom_call" | custom-call | tf_op jit(solution)/shard_map/pallas_call | solution.py:63
  227.9 5.1 %bitcast_add_fusion = f32[2048,512]{0,1:T(8,128)} fusion(f32[4,128,2048]{2,1,0:T(8,128)} %fusion.3, bf16[128,2048]{1,0:T(8,128)(2,1)S(1)} %copy-done.2, f32[128,512]{1,0:T(8,128)S(1)} %copy.17, f32[136,512]{1,0:T(8,128)} %shard_map.79, f32[128,512]{1,0:T(8,128)S(1)} %copy-done.4, f32[512]{0:T(512)S(1)} %copy-done.7), kind=kOutput, calls=%fused_computation.1 | convolution fusion | flops 270925824 | bytes 9701376 | tf_op jit(solution)/shard_map/dot_general | solution.py:233
  233.0 0.0 reduce-scatter.2.cloned.1.call-update
  233.0 0.7 slice.57
  233.7 0.6 scatter.9.x_ref
  234.3 6.7 %shard_map.80 = f32[8,128]{1,0:T(8,128)} custom-call(f32[8,128]{1,0:T(8,128)} %scatter.9.x_ref), custom_call_target="tpu_custom_call" | custom-call | tf_op jit(solution)/shard_map/pallas_call | solution.py:63
  241.0 1.2 multiply_bitcast_fusion
  242.2 46.5 %reduce-scatter.2.cloned.1.call-done = f32[512,512]{0,1:T(8,128)} async-done(((f32[2048,512]{0,1:T(8,128)}), f32[512,512]{0,1:T(8,128)}) %reduce-scatter.2.cloned.1.call-update) | async-done | bytes 1048592 | tf_op jit(solution)/shard_map/reduce_scatter | solution.py:236
  288.7 1.3 convert_element_type.33
  290.0 1.0 copy.16
  (24 shorter events, 0.1 us)
Async XLA Ops:
  7.2 3.3 %copy-start = (bf16[512,2048]{1,0:T(8,128)(2,1)S(1)}, bf16[512,2048]{1,0:T(8,128)(2,1)}, u32[]{:S(2)}) copy-start(bf16[512,2048]{1,0:T(8,128)(2,1)} %param.11) | copy-start | bytes 6291460
  7.2 3.3 %copy-start.2 = (bf16[128,2048]{1,0:T(8,128)(2,1)S(1)}, bf16[128,2048]{1,0:T(8,128)(2,1)}, u32[]{:S(2)}) copy-start(bf16[128,2048]{1,0:T(8,128)(2,1)} %param.10) | copy-start | bytes 1572868
  7.2 281.5 %reduce-scatter.2.cloned.1.call-start = ((), (), s32[]{:S(2)}) async-start(), calls=%async_computation.1 | async-start | bytes 5242880 | tf_op jit(solution)/shard_map/reduce_scatter | solution.py:236
  10.5 12.0 %copy-start.8 = (s32[4]{0:T(128)S(1)}, s32[4]{0:T(128)}, u32[]{:S(2)}) copy-start(s32[4]{0:T(128)} %param.15) | copy-start | bytes 52
  10.5 12.1 %copy-start.7 = (f32[512]{0:T(512)S(1)}, f32[512]{0:T(512)}, u32[]{:S(2)}) copy-start(f32[512]{0:T(512)} %param.12) | copy-start | bytes 6148
  27.5 176.5 %copy-start.3 = (f32[128,2048]{1,0:T(8,128)S(1)}, f32[128,2048]{1,0:T(8,128)}, u32[]{:S(2)}) copy-start(f32[128,2048]{1,0:T(8,128)} %convert_element_type.30) | copy-start | bytes 3145732
  27.5 176.5 %copy-start.6 = (f32[2048]{0:T(1024)S(1)}, f32[2048]{0:T(1024)}, u32[]{:S(2)}) copy-start(f32[2048]{0:T(1024)} %param.13) | copy-start | bytes 24580
  211.7 3.6 %copy-start.5 = (f32[128,512]{0,1:T(8,128)S(1)}, f32[128,512]{0,1:T(8,128)}, u32[]{:S(2)}) copy-start(f32[128,512]{0,1:T(8,128)} %copy.19) | copy-start | bytes 786436
  215.3 4.5 %copy-start.1 = (bf16[4,128,2048]{2,1,0:T(8,128)(2,1)S(1)}, bf16[4,128,2048]{2,1,0:T(8,128)(2,1)}, u32[]{:S(2)}) copy-start(bf16[4,128,2048]{2,1,0:T(8,128)(2,1)} %gather_fusion) | copy-start | bytes 6291460
  219.8 8.1 %copy-start.4 = (f32[128,512]{1,0:T(8,128)S(1)}, f32[128,512]{1,0:T(8,128)}, u32[]{:S(2)}) copy-start(f32[128,512]{1,0:T(8,128)} %shard_map.77) | copy-start | bytes 786436
Sparse Core Ops, SparseCore 0:
  233.1 55.5 reduce-scatter.1

commit v3 on v2

--- a/solution.py
+++ b/solution.py
@@ -38,6 +38,89 @@
         s = (pos + n - d) % n
         remote(src_of(s), slot_of(s), send_sems.at[s], recv_sems.at[s], dev_of(s)).wait_recv()
     return sends
+
+
+def ring_reduce_scatter(n, pos, dev_of, src, recv, acc, sems, put):
+    half = src.shape[1] // 2
+    dirs = (1, n - 1)
+    sends = []
+    for s in range(n - 1):
+        for h, dr in enumerate(dirs):
+            k = (pos + (s + 1) * (n - dr)) % n
+            source = src.at[k, pl.ds(h * half, half)] if s == 0 else acc.at[h, s - 1]
+            cp = remote(source, recv.at[h, s], sems.at[h, 0, s], sems.at[h, 1, s], dev_of((pos + dr) % n))
+            cp.start()
+            sends.append(cp)
+        for h, dr in enumerate(dirs):
+            k2 = (pos + (s + 2) * (n - dr)) % n
+            own = src.at[k2, pl.ds(h * half, half)]
+            remote(own, recv.at[h, s], sems.at[h, 0, s], sems.at[h, 1, s],
+                   dev_of((pos + n - dr) % n)).wait_recv()
+            new = recv[h, s] + own[...]
+            if s < n - 2:
+                acc[h, s] = new
+            else:
+                put(h, new)
+    return sends
+
+
+def ring_all_gather(n, pos, dev_of, mine, dst, sems):
+    half = mine.shape[0] // 2
+    dirs = (1, n - 1)
+    dst[pos] = mine[...]
+    sends = []
+    for s in range(n - 1):
+        for h, dr in enumerate(dirs):
+            k = (pos + s * (n - dr)) % n
+            rows = pl.ds(h * half, half)
+            source = mine.at[rows] if s == 0 else dst.at[k, rows]
+            cp = remote(source, dst.at[k, rows], sems.at[h, 0, s], sems.at[h, 1, s], dev_of((pos + dr) % n))
+            cp.start()
+            sends.append(cp)
+        for h, dr in enumerate(dirs):
+            k2 = (pos + (s + 1) * (n - dr)) % n
+            rows = pl.ds(h * half, half)
+            remote(mine.at[rows], dst.at[k2, rows], sems.at[h, 0, s], sems.at[h, 1, s],
+                   dev_of((pos + n - dr) % n)).wait_recv()
+    return sends
+
+
+def ring_sum_kernel(axis_names, axis, n, x_ref, out_ref, recv, acc, sems):
+    me = lax.axis_index(axis)
+
+    def dev_of(c):
+        return device_on(axis_names, {axis: c})
+
+    barrier = pltpu.get_barrier_semaphore()
+    for d in range(1, n):
+        pl.semaphore_signal(barrier, 1, device_id=dev_of((me + d) % n), device_id_type=MESH_ID)
+    pl.semaphore_wait(barrier, n - 1)
+    half = x_ref.shape[1] // 2
+
+    def put(h, value):
+        out_ref[pl.ds(h * half, half)] = value.astype(out_ref.dtype)
+
+    sends = ring_reduce_scatter(n, me, dev_of, x_ref, recv, acc, sems, put)
+    for cp in sends:
+        cp.wait_send()
+
+
+def ring_sum_scatter(x, axis_names, axis, n, cid, out_dtype):
+    _, rows, width = x.shape
+    return pl.pallas_call(
+        functools.partial(ring_sum_kernel, axis_names, axis, n),
+        out_shape=jax.ShapeDtypeStruct((rows, width), out_dtype),
+        in_specs=[pl.BlockSpec(memory_space=pltpu.VMEM)],
+        out_specs=pl.BlockSpec(memory_space=pltpu.VMEM),
+        scratch_shapes=[
+            pltpu.VMEM((2, n - 1, rows // 2, width), x.dtype),
+            pltpu.VMEM((2, max(n - 2, 1), rows // 2, width), x.dtype),
+            pltpu.SemaphoreType.DMA((2, 2, n - 1)),
+        ],
+        compiler_params=pltpu.CompilerParams(
+            collective_id=cid, has_side_effects=True, vmem_limit_bytes=48 * 1024 * 1024
+        ),
+    )(x)
 
 
 def axis_sum_kernel(axis_names, axis, n, x_ref, out_ref, slots, send_sem, recv_sem):
@@ -74,8 +157,8 @@
     )(x)
 
 
-def lat_sum_kernel(axis_names, ny, nlo, nhi, x_ref, out_ref, recv1, recv2, recv3, part3, part2, part1,
-                   ag2, ag1, sems):
+def lat_sum_kernel(axis_names, ny, nlo, nhi, x_ref, out_ref, recv1, acc1, recv2, recv3, part3, part2,
+                   part1, ag2, ag1, sems, ring_sems):
     lat = lax.axis_index("lat")
     my_y = lat % ny
     my_z = lat // ny
@@ -109,9 +192,12 @@
             total = total + slots[s]
         return total
 
-    sends = gather_phase(ny, my_y, y_dev, lambda c: x_ref.at[c], lambda c: recv1.at[c],
-                         sems.at[0, 0], sems.at[0, 1])
-    part1[...] = summed(recv1, ny)
+    half = rows // 2
+
+    def put(h, value):
+        part1[pl.ds(h * half, half)] = value
+
+    sends = ring_reduce_scatter(ny, my_y, y_dev, x_ref, recv1, acc1, ring_sems.at[0], put)
     for cp in sends:
         cp.wait_send()
     sends = gather_phase(nlo, my_lo, lo_dev, lambda c: part1.at[rows_of(c, c2)], lambda c: recv2.at[c],
@@ -132,8 +218,7 @@
                          sems.at[4, 0], sems.at[4, 1])
     for cp in sends:
         cp.wait_send()
-    sends = gather_phase(ny, my_y, y_dev, lambda c: ag1, lambda c: out_ref.at[c],
-                         sems.at[5, 0], sems.at[5, 1])
+    sends = ring_all_gather(ny, my_y, y_dev, ag1, out_ref, ring_sems.at[1])
     for cp in sends:
         cp.wait_send()
 
@@ -155,7 +240,8 @@
         in_specs=[pl.BlockSpec(memory_space=pltpu.VMEM)],
         out_specs=pl.BlockSpec(memory_space=pltpu.VMEM),
         scratch_shapes=[
-            pltpu.VMEM((ny, rows, width), f32),
+            pltpu.VMEM((2, ny - 1, rows // 2, width), f32),
+            pltpu.VMEM((2, max(ny - 2, 1), rows // 2, width), f32),
             pltpu.VMEM((nlo, c2, width), f32),
             pltpu.VMEM((nhi, c3, width), f32),
             pltpu.VMEM((c3, width), f32),
@@ -164,6 +250,7 @@
             pltpu.VMEM((c2, width), f32),
             pltpu.VMEM((rows, width), f32),
             pltpu.SemaphoreType.DMA((6, 2, most)),
+            pltpu.SemaphoreType.DMA((2, 2, 2, ny - 1)),
         ],
         compiler_params=pltpu.CompilerParams(
             collective_id=cid, has_side_effects=True, vmem_limit_bytes=48 * 1024 * 1024
@@ -233,13 +320,14 @@
     encode_term = lax.dot_general(
         resid, g_pre, (((0,), (0,)), ((), ())), preferred_element_type=jnp.float32
     )
-    grad_share = lax.psum_scatter(
-        decode_term.reshape(half_width, lat_count) + encode_term,
-        "tok",
-        scatter_dimension=0,
-        tiled=True,
-    )
-    return (level_losses, grad_share.astype(jnp.bfloat16))
+    tok_count = lax.axis_size("tok")
+    grad_share = ring_sum_scatter(
+        (decode_term.reshape(half_width, lat_count) + encode_term).reshape(
+            tok_count, half_width // tok_count, lat_count
+        ),
+        axis_names, "tok", tok_count, 4, jnp.bfloat16,
+    )
+    return (level_losses, grad_share)
 
 
 def solution(mesh):

time: 298 us -> 264 us (0.89)
  the two profiles are of different devices: /device:TPU:1 before, /device:TPU:32 now
where the time goes in v3:
time: 264 us; the launch traced here: 263 us
  Pallas kernels  223 us (84%)
  matrix products  16.9 us (6%)
  local copies, waits for them, and re-layouts  15.1 us (6%)
  other arithmetic  7.43 us (3%)
    pallas_call x1, Pallas kernels, lat_sum(): pl.pallas_call(functools.partial(lat_sum_kernel, axis_names, ny, nlo, nhi...  165 us
    pallas_call x1, Pallas kernels, ring_sum_scatter(): pl.pallas_call(functools.partial(ring_sum_kernel, axis_names, axis, n), o...  42.6 us
    pallas_call x3, Pallas kernels, axis_sum(): pl.pallas_call(functools.partial(axis_sum_kernel, axis_names, axis, n), o...  15.2 us
    add x1, local copies, waits for them, and re-layouts, body(): decode_term.reshape(half_width, lat_count) + encode_term  5.34 us

profile of v3, /device:TPU:32, one launch (start us, length us, event | category | flops | bytes accessed | tf_op | source)
XLA Modules:
  0.0 263.0 jit_solution(13783423014571372214)
XLA Ops:
  0.6 0.0 copy-start
  0.7 0.9 compare_reduce_fusion
  1.6 0.1 copy.17
  1.8 0.5 copy-done
  2.2 2.6 fusion.41.x_ref
  4.8 3.9 %shard_map.77 = f32[128,512]{1,0:T(8,128)} custom-call(f32[128,512]{1,0:T(8,128)} %fusion.41.x_ref), custom_call_target="tpu_custom_call" | custom-call | tf_op jit(solution)/shard_map/pallas_call | solution.py:146
  8.8 1.1 multiply_convert_fusion.1
  9.9 0.1 broadcast_compare_fusion
  10.0 3.2 %fusion.x_ref = f32[4,128,2048]{2,1,0:T(8,128)} fusion(bf16[512,2048]{1,0:T(8,128)(2,1)S(1)} %copy-done, pred[4,512]{1,0:T(4,128)(4,1)S(1)} %broadcast_compare_fusion, bf16[128,512]{1,0:T(8,128)(2,1)S(1)} %get-tuple-element.28), kind=kOutput, calls=%fused_computation.5 | convolution fusion | flops 1074003968 | bytes 6424576 | tf_op jit(solution)/shard_map/dot_general | solution.py:286
  13.2 165.0 %shard_map.78 = f32[4,128,2048]{2,1,0:T(8,128)S(1)} custom-call(f32[4,128,2048]{2,1,0:T(8,128)} %fusion.x_ref), custom_call_target="tpu_custom_call" | custom-call | tf_op jit(solution)/shard_map/pallas_call | solution.py:237
  178.2 0.1 convert_element_type.27
  178.3 1.1 multiply_reduce_fusion
  179.5 0.4 fusion.2
  179.9 0.1 slice.92
  180.0 1.6 pad_maximum_fusion
  181.6 0.2 convert_reduce_fusion
  181.8 3.6 %gather_fusion = bf16[4,128,2048]{2,1,0:T(8,128)(2,1)} fusion(bf16[4,128,2048]{2,1,0:T(8,128)(2,1)} %pad_maximum_fusion, s32[1024]{0:T(1024)S(1)} %pad_clamp_fusion), kind=kCustom, calls=%fused_computation | custom fusion | bytes 4194320 | tf_op jit(solution)/shard_map/jit(_take)/gather | solution.py:303
  185.3 0.1 copy.19
  185.5 4.4 %fusion.3 = f32[4,128,2048]{2,1,0:T(8,128)} fusion(bf16[4,128,2048]{2,1,0:T(8,128)(2,1)} %gather_fusion, pred[4]{0:T(512)(128)(4,1)S(1)} %compare_and_fusion, f32[128,4,128]{0,2,1:T(8,128)S(1)} %bitcast.29, f32[128,4]{0,1:T(4,128)S(1)} %convert_element_type.25), kind=kOutput, calls=%fused_computation.13 | convolution fusion | flops 269615104 | bytes 6555652 | tf_op jit(solution)/shard_map/ktd,tkc->dkc/dot_general | solution.py:319
  189.9 1.5 fusion.4
  191.5 1.1 copy.18
  192.6 0.7 select_maximum_fusion.x_ref
  193.3 4.0 %shard_map.79 = f32[136,512]{1,0:T(8,128)} custom-call(f32[136,512]{1,0:T(8,128)} %select_maximum_fusion.x_ref), custom_call_target="tpu_custom_call" | custom-call | tf_op jit(solution)/shard_map/pallas_call | solution.py:146
  197.3 5.1 %bitcast_add_fusion = f32[2048,512]{0,1:T(8,128)} fusion(f32[4,128,2048]{2,1,0:T(8,128)} %fusion.3, bf16[128,2048]{1,0:T(8,128)(2,1)S(1)} %copy-done.3, f32[128,512]{1,0:T(8,128)S(1)} %copy.17, f32[136,512]{1,0:T(8,128)} %shard_map.79, f32[128,512]{1,0:T(8,128)S(1)} %copy-done.4, f32[512]{0:T(512)S(1)} %copy-done.6), kind=kOutput, calls=%fused_computation.1 | convolution fusion | flops 270925824 | bytes 9701376 | tf_op jit(solution)/shard_map/dot_general | solution.py:320
  202.5 5.3 %copy.16 = f32[2048,512]{1,0:T(8,128)} copy(f32[2048,512]{0,1:T(8,128)} %bitcast_add_fusion) | data formatting | bytes 8388608 | tf_op jit(solution)/shard_map/add | solution.py:325
  207.8 2.2 copy-done.1
  210.0 42.6 %shard_map.81 = bf16[512,512]{1,0:T(8,128)(2,1)S(1)} custom-call(f32[4,512,512]{2,1,0:T(8,128)S(1)} %bitcast.28), custom_call_target="tpu_custom_call" | custom-call | tf_op jit(solution)/shard_map/pallas_call | solution.py:110
  252.6 0.7 slice.57
  253.2 0.6 scatter.9.x_ref
  253.8 7.2 %shard_map.80 = f32[8,128]{1,0:T(8,128)} custom-call(f32[8,128]{1,0:T(8,128)} %scatter.9.x_ref), custom_call_target="tpu_custom_call" | custom-call | tf_op jit(solution)/shard_map/pallas_call | solution.py:146
  261.0 1.2 multiply_bitcast_fusion
  262.2 0.8 copy.21
  (20 shorter events, 0.1 us)
Async XLA Ops:
  0.6 1.6 copy-start
  1.6 7.2 %copy-start.6 = (f32[512]{0:T(512)S(1)}, f32[512]{0:T(512)}, u32[]{:S(2)}) copy-start(f32[512]{0:T(512)} %param.12) | copy-start | bytes 6148
  2.2 7.6 %copy-start.7 = (s32[4]{0:T(128)S(1)}, s32[4]{0:T(128)}, u32[]{:S(2)}) copy-start(s32[4]{0:T(128)} %param.15) | copy-start | bytes 52
  13.2 165.0 %copy-start.3 = (bf16[128,2048]{1,0:T(8,128)(2,1)S(1)}, bf16[128,2048]{1,0:T(8,128)(2,1)}, u32[]{:S(2)}) copy-start(bf16[128,2048]{1,0:T(8,128)(2,1)} %param.10) | copy-start | bytes 1572868
  13.2 165.2 %copy-start.5 = (f32[2048]{0:T(1024)S(1)}, f32[2048]{0:T(1024)}, u32[]{:S(2)}) copy-start(f32[2048]{0:T(1024)} %param.13) | copy-start | bytes 24580
  185.5 4.5 %copy-start.2 = (bf16[4,128,2048]{2,1,0:T(8,128)(2,1)S(1)}, bf16[4,128,2048]{2,1,0:T(8,128)(2,1)}, u32[]{:S(2)}) copy-start(bf16[4,128,2048]{2,1,0:T(8,128)(2,1)} %gather_fusion) | copy-start | bytes 6291460
  189.9 7.4 %copy-start.4 = (f32[128,512]{1,0:T(8,128)S(1)}, f32[128,512]{1,0:T(8,128)}, u32[]{:S(2)}) copy-start(f32[128,512]{1,0:T(8,128)} %shard_map.77) | copy-start | bytes 786436
  207.8 2.2 copy-start.1

commit v4 on v3

--- a/solution.py
+++ b/solution.py
@@ -157,14 +157,89 @@
     )(x)
 
 
-def lat_sum_kernel(axis_names, ny, nlo, nhi, x_ref, out_ref, recv1, acc1, recv2, recv3, part3, part2,
-                   part1, ag2, ag1, sems, ring_sems):
+def ring_rs_steps(n, pos, dev_of, src, recv, acc, sems, put, sends):
+    half = src.shape[1] // 2
+    dirs = (1, n - 1)
+    steps = []
+    for s in range(n - 1):
+        def start(s=s):
+            for h, dr in enumerate(dirs):
+                k = (pos + (s + 1) * (n - dr)) % n
+                source = src.at[k, pl.ds(h * half, half)] if s == 0 else acc.at[h, s - 1]
+                cp = remote(source, recv.at[h, s], sems.at[h, 0, s], sems.at[h, 1, s], dev_of((pos + dr) % n))
+                cp.start()
+                sends.append(cp)
+
+        def finish(s=s):
+            for h, dr in enumerate(dirs):
+                k2 = (pos + (s + 2) * (n - dr)) % n
+                own = src.at[k2, pl.ds(h * half, half)]
+                remote(own, recv.at[h, s], sems.at[h, 0, s], sems.at[h, 1, s],
+                       dev_of((pos + n - dr) % n)).wait_recv()
+                new = recv[h, s] + own[...]
+                if s < n - 2:
+                    acc[h, s] = new
+                else:
+                    put(h, new)
+
+        steps.append((start, finish))
+    return steps
+
+
+def ring_ag_steps(n, pos, dev_of, mine, dst, sems, sends):
+    half = mine.shape[0] // 2
+    dirs = (1, n - 1)
+    steps = []
+    for s in range(n - 1):
+        def start(s=s):
+            if s == 0:
+                dst[pos] = mine[...]
+            for h, dr in enumerate(dirs):
+                k = (pos + s * (n - dr)) % n
+                rows = pl.ds(h * half, half)
+                source = mine.at[rows] if s == 0 else dst.at[k, rows]
+                cp = remote(source, dst.at[k, rows], sems.at[h, 0, s], sems.at[h, 1, s], dev_of((pos + dr) % n))
+                cp.start()
+                sends.append(cp)
+
+        def finish(s=s):
+            for h, dr in enumerate(dirs):
+                k2 = (pos + (s + 1) * (n - dr)) % n
+                rows = pl.ds(h * half, half)
+                remote(mine.at[rows], dst.at[k2, rows], sems.at[h, 0, s], sems.at[h, 1, s],
+                       dev_of((pos + n - dr) % n)).wait_recv()
+
+        steps.append((start, finish))
+    return steps
+
+
+def direct_step(n, pos, dev_of, src_of, slot_of, send_sems, recv_sems, sends, after):
+    def start():
+        for d in range(1, n):
+            c = (pos + d) % n
+            cp = remote(src_of(c), slot_of(pos), send_sems.at[c], recv_sems.at[pos], dev_of(c))
+            cp.start()
+            sends.append(cp)
+        slot_of(pos)[...] = src_of(pos)[...]
+
+    def finish():
+        for d in range(1, n):
+            s = (pos + n - d) % n
+            remote(src_of(s), slot_of(s), send_sems.at[s], recv_sems.at[s], dev_of(s)).wait_recv()
+        after()
+
+    return [(start, finish)]
+
+
+def lat_sum_kernel(axis_names, ny, nlo, nhi, x_ref, out_ref, recv1, acc1, part1, recv2, part2, recv3, part3,
+                   ag2, ag1, ring_sems, sems):
     lat = lax.axis_index("lat")
     my_y = lat % ny
     my_z = lat // ny
     my_lo = my_z % nlo
     my_hi = my_z // nlo
     rows = x_ref.shape[1]
+    cols = part1.shape[-1]
     c2 = rows // nlo
     c3 = c2 // nhi
 
@@ -192,33 +267,49 @@
             total = total + slots[s]
         return total
 
-    half = rows // 2
-
-    def put(h, value):
-        part1[pl.ds(h * half, half)] = value
-
-    sends = ring_reduce_scatter(ny, my_y, y_dev, x_ref, recv1, acc1, ring_sems.at[0], put)
-    for cp in sends:
-        cp.wait_send()
-    sends = gather_phase(nlo, my_lo, lo_dev, lambda c: part1.at[rows_of(c, c2)], lambda c: recv2.at[c],
-                         sems.at[1, 0], sems.at[1, 1])
-    part2[...] = summed(recv2, nlo)
-    for cp in sends:
-        cp.wait_send()
-    sends = gather_phase(nhi, my_hi, hi_dev, lambda c: part2.at[rows_of(c, c3)], lambda c: recv3.at[c],
-                         sems.at[2, 0], sems.at[2, 1])
-    part3[...] = summed(recv3, nhi)
-    for cp in sends:
-        cp.wait_send()
-    sends = gather_phase(nhi, my_hi, hi_dev, lambda c: part3, lambda c: ag2.at[rows_of(c, c3)],
-                         sems.at[3, 0], sems.at[3, 1])
-    for cp in sends:
-        cp.wait_send()
-    sends = gather_phase(nlo, my_lo, lo_dev, lambda c: ag2, lambda c: ag1.at[rows_of(c, c2)],
-                         sems.at[4, 0], sems.at[4, 1])
-    for cp in sends:
-        cp.wait_send()
-    sends = ring_all_gather(ny, my_y, y_dev, ag1, out_ref, ring_sems.at[1])
+    sends = []
+    streams = []
+    for q in range(2):
+        width = pl.ds(q * cols, cols)
+        half = rows // 2
+
+        def put(h, value, q=q, half=half):
+            part1[q, pl.ds(h * half, half)] = value
+
+        def sum_lo(q=q):
+            part2[q] = summed(recv2.at[q], nlo)
+
+        def sum_hi(q=q):
+            part3[q] = summed(recv3.at[q], nhi)
+
+        steps = []
+        steps += ring_rs_steps(ny, my_y, y_dev, x_ref.at[:, :, width], recv1.at[q], acc1.at[q],
+                               ring_sems.at[q, 0], put, sends)
+        steps += direct_step(nlo, my_lo, lo_dev, lambda c, q=q: part1.at[q, rows_of(c, c2)],
+                             lambda c, q=q: recv2.at[q, c], sems.at[q, 0, 0], sems.at[q, 0, 1], sends, sum_lo)
+        steps += direct_step(nhi, my_hi, hi_dev, lambda c, q=q: part2.at[q, rows_of(c, c3)],
+                             lambda c, q=q: recv3.at[q, c], sems.at[q, 1, 0], sems.at[q, 1, 1], sends, sum_hi)
+        steps += direct_step(nhi, my_hi, hi_dev, lambda c, q=q: part3.at[q],
+                             lambda c, q=q: ag2.at[q, rows_of(c, c3)], sems.at[q, 2, 0], sems.at[q, 2, 1],
+                             sends, lambda: None)
+        steps += direct_step(nlo, my_lo, lo_dev, lambda c, q=q: ag2.at[q],
+                             lambda c, q=q: ag1.at[q, rows_of(c, c2)], sems.at[q, 3, 0], sems.at[q, 3, 1],
+                             sends, lambda: None)
+        steps += ring_ag_steps(ny, my_y, y_dev, ag1.at[q], out_ref.at[:, :, width], ring_sems.at[q, 1], sends)
+        streams.append(steps)
+
+    lag = ny - 1
+    total_slots = len(streams[0]) + lag
+    for slot in range(total_slots):
+        active = []
+        for q, offset in ((0, 0), (1, lag)):
+            i = slot - offset
+            if 0 <= i < len(streams[q]):
+                active.append(streams[q][i])
+        for start, _ in active:
+            start()
+        for _, finish in active:
+            finish()
     for cp in sends:
         cp.wait_send()
 
@@ -229,28 +320,29 @@
     nlo = 4 if nz % 4 == 0 else nz
     nhi = nz // nlo
     chunks, rows, width = x.shape
-    assert chunks == ny and rows % (8 * nz) == 0
+    assert chunks == ny and rows % (8 * nz) == 0 and width % 256 == 0
+    cols = width // 2
     c2 = rows // nlo
     c3 = c2 // nhi
     f32 = jnp.float32
-    most = max(ny, nlo, nhi)
+    most = max(nlo, nhi)
     return pl.pallas_call(
         functools.partial(lat_sum_kernel, axis_names, ny, nlo, nhi),
         out_shape=jax.ShapeDtypeStruct(x.shape, x.dtype),
         in_specs=[pl.BlockSpec(memory_space=pltpu.VMEM)],
         out_specs=pl.BlockSpec(memory_space=pltpu.VMEM),
         scratch_shapes=[
-            pltpu.VMEM((2, ny - 1, rows // 2, width), f32),
-            pltpu.VMEM((2, max(ny - 2, 1), rows // 2, width), f32),
-            pltpu.VMEM((nlo, c2, width), f32),
-            pltpu.VMEM((nhi, c3, width), f32),
-            pltpu.VMEM((c3, width), f32),
-            pltpu.VMEM((c2, width), f32),
-            pltpu.VMEM((rows, width), f32),
-            pltpu.VMEM((c2, width), f32),
-            pltpu.VMEM((rows, width), f32),
-            pltpu.SemaphoreType.DMA((6, 2, most)),
-            pltpu.SemaphoreType.DMA((2, 2, 2, ny - 1)),
+            pltpu.VMEM((2, 2, ny - 1, rows // 2, cols), f32),
+            pltpu.VMEM((2, 2, max(ny - 2, 1), rows // 2, cols), f32),
+            pltpu.VMEM((2, rows, cols), f32),
+            pltpu.VMEM((2, nlo, c2, cols), f32),
+            pltpu.VMEM((2, c2, cols), f32),
+            pltpu.VMEM((2, nhi, c3, cols), f32),
+            pltpu.VMEM((2, c3, cols), f32),
+            pltpu.VMEM((2, c2, cols), f32),
+            pltpu.VMEM((2, rows, cols), f32),
+            pltpu.SemaphoreType.DMA((2, 2, 2, 2, ny - 1)),
+            pltpu.SemaphoreType.DMA((2, 4, 2, most)),
         ],
         compiler_params=pltpu.CompilerParams(
             collective_id=cid, has_side_effects=True, vmem_limit_bytes=48 * 1024 * 1024

time: 264 us -> 240 us (0.909)
  the two profiles are of different devices: /device:TPU:32 before, /device:TPU:1 now
where the time goes in v4:
time: 240 us; the launch traced here: 235 us
  Pallas kernels  195 us (81%)
  matrix products  16.9 us (7%)
  local copies, waits for them, and re-layouts  15.1 us (6%)
  other arithmetic  7.43 us (3%)
    pallas_call x1, Pallas kernels, lat_sum(): pl.pallas_call(functools.partial(lat_sum_kernel, axis_names, ny, nlo, nhi...  129 us
    pallas_call x1, Pallas kernels, ring_sum_scatter(): pl.pallas_call(functools.partial(ring_sum_kernel, axis_names, axis, n), o...  39.5 us
    pallas_call x3, Pallas kernels, axis_sum(): pl.pallas_call(functools.partial(axis_sum_kernel, axis_names, axis, n), o...  26.1 us
    add x1, local copies, waits for them, and re-layouts, body(): decode_term.reshape(half_width, lat_count) + encode_term  5.34 us
    dot_general x1, matrix products, body(): lax.dot_general(resid, g_pre, (((0,), (0,)), ((), ())), preferred_element...  5.14 us

profile of v4, /device:TPU:1, one launch (start us, length us, event | category | flops | bytes accessed | tf_op | source)
XLA Modules:
  0.0 235.1 jit_solution(5733932520145848799)
XLA Ops:
  0.6 0.0 copy-start
  0.7 0.9 compare_reduce_fusion
  1.6 0.1 copy.17
  1.8 0.5 copy-done
  2.2 2.6 %fusion.41.x_ref = f32[128,512]{1,0:T(8,128)} fusion(bf16[128,2048]{1,0:T(8,128)(2,1)} %param.10, bf16[512,2048]{1,0:T(8,128)(2,1)S(1)} %copy-done), kind=kOutput, calls=%fused_computation.70 | convolution fusion | flops 268435456 | bytes 2883584 | tf_op jit(solution)/shard_map/dot_general | solution.py:363
  4.8 10.4 %shard_map.77 = f32[128,512]{1,0:T(8,128)} custom-call(f32[128,512]{1,0:T(8,128)} %fusion.41.x_ref), custom_call_target="tpu_custom_call" | custom-call | tf_op jit(solution)/shard_map/pallas_call | solution.py:146
  15.3 1.1 multiply_convert_fusion.1
  16.4 0.1 broadcast_compare_fusion
  16.4 3.2 %fusion.x_ref = f32[4,128,2048]{2,1,0:T(8,128)} fusion(bf16[512,2048]{1,0:T(8,128)(2,1)S(1)} %copy-done, pred[4,512]{1,0:T(4,128)(4,1)S(1)} %broadcast_compare_fusion, bf16[128,512]{1,0:T(8,128)(2,1)S(1)} %get-tuple-element.28), kind=kOutput, calls=%fused_computation.5 | convolution fusion | flops 1074003968 | bytes 6424576 | tf_op jit(solution)/shard_map/dot_general | solution.py:378
  19.6 129.3 %shard_map.78 = f32[4,128,2048]{2,1,0:T(8,128)S(1)} custom-call(f32[4,128,2048]{2,1,0:T(8,128)} %fusion.x_ref), custom_call_target="tpu_custom_call" | custom-call | tf_op jit(solution)/shard_map/pallas_call | solution.py:329
  148.9 0.1 convert_element_type.27
  149.0 1.1 multiply_reduce_fusion
  150.2 0.4 fusion.2
  150.6 0.1 slice.92
  150.7 1.6 pad_maximum_fusion
  152.3 0.2 convert_reduce_fusion
  152.5 3.6 %gather_fusion = bf16[4,128,2048]{2,1,0:T(8,128)(2,1)} fusion(bf16[4,128,2048]{2,1,0:T(8,128)(2,1)} %pad_maximum_fusion, s32[1024]{0:T(1024)S(1)} %pad_clamp_fusion), kind=kCustom, calls=%fused_computation | custom fusion | bytes 4194320 | tf_op jit(solution)/shard_map/jit(_take)/gather | solution.py:395
  156.0 0.1 copy.19
  156.2 4.4 %fusion.3 = f32[4,128,2048]{2,1,0:T(8,128)} fusion(bf16[4,128,2048]{2,1,0:T(8,128)(2,1)} %gather_fusion, pred[4]{0:T(512)(128)(4,1)S(1)} %compare_and_fusion, f32[128,4,128]{0,2,1:T(8,128)S(1)} %bitcast.29, f32[128,4]{0,1:T(4,128)S(1)} %convert_element_type.25), kind=kOutput, calls=%fused_computation.13 | convolution fusion | flops 269615104 | bytes 6555652 | tf_op jit(solution)/shard_map/ktd,tkc->dkc/dot_general | solution.py:411
  160.6 1.5 fusion.4
  162.2 1.1 copy.18
  163.3 0.7 select_maximum_fusion.x_ref
  164.0 9.6 %shard_map.79 = f32[136,512]{1,0:T(8,128)} custom-call(f32[136,512]{1,0:T(8,128)} %select_maximum_fusion.x_ref), custom_call_target="tpu_custom_call" | custom-call | tf_op jit(solution)/shard_map/pallas_call | solution.py:146
  173.6 5.1 %bitcast_add_fusion = f32[2048,512]{0,1:T(8,128)} fusion(f32[4,128,2048]{2,1,0:T(8,128)} %fusion.3, bf16[128,2048]{1,0:T(8,128)(2,1)S(1)} %copy-done.3, f32[128,512]{1,0:T(8,128)S(1)} %copy.17, f32[136,512]{1,0:T(8,128)} %shard_map.79, f32[128,512]{1,0:T(8,128)S(1)} %copy-done.4, f32[512]{0:T(512)S(1)} %copy-done.6), kind=kOutput, calls=%fused_computation.1 | convolution fusion | flops 270925824 | bytes 9701376 | tf_op jit(solution)/shard_map/dot_general | solution.py:412
  178.8 5.3 %copy.16 = f32[2048,512]{1,0:T(8,128)} copy(f32[2048,512]{0,1:T(8,128)} %bitcast_add_fusion) | data formatting | bytes 8388608 | tf_op jit(solution)/shard_map/add | solution.py:417
  184.1 2.2 copy-done.1
  186.3 39.5 %shard_map.81 = bf16[512,512]{1,0:T(8,128)(2,1)S(1)} custom-call(f32[4,512,512]{2,1,0:T(8,128)S(1)} %bitcast.28), custom_call_target="tpu_custom_call" | custom-call | tf_op jit(solution)/shard_map/pallas_call | solution.py:110
  225.8 0.7 slice.57
  226.5 0.6 scatter.9.x_ref
  227.1 6.1 %shard_map.80 = f32[8,128]{1,0:T(8,128)} custom-call(f32[8,128]{1,0:T(8,128)} %scatter.9.x_ref), custom_call_target="tpu_custom_call" | custom-call | tf_op jit(solution)/shard_map/pallas_call | solution.py:146
  233.1 1.2 multiply_bitcast_fusion
  234.3 0.8 copy.21
  (20 shorter events, 0.1 us)
Async XLA Ops:
  0.6 1.6 copy-start
  1.6 13.7 %copy-start.6 = (f32[512]{0:T(512)S(1)}, f32[512]{0:T(512)}, u32[]{:S(2)}) copy-start(f32[512]{0:T(512)} %param.12) | copy-start | bytes 6148
  2.2 14.1 %copy-start.7 = (s32[4]{0:T(128)S(1)}, s32[4]{0:T(128)}, u32[]{:S(2)}) copy-start(s32[4]{0:T(128)} %param.15) | copy-start | bytes 52
  19.6 129.3 %copy-start.3 = (bf16[128,2048]{1,0:T(8,128)(2,1)S(1)}, bf16[128,2048]{1,0:T(8,128)(2,1)}, u32[]{:S(2)}) copy-start(bf16[128,2048]{1,0:T(8,128)(2,1)} %param.10) | copy-start | bytes 1572868
  19.6 129.4 %copy-start.5 = (f32[2048]{0:T(1024)S(1)}, f32[2048]{0:T(1024)}, u32[]{:S(2)}) copy-start(f32[2048]{0:T(1024)} %param.13) | copy-start | bytes 24580
  156.2 4.5 %copy-start.2 = (bf16[4,128,2048]{2,1,0:T(8,128)(2,1)S(1)}, bf16[4,128,2048]{2,1,0:T(8,128)(2,1)}, u32[]{:S(2)}) copy-start(bf16[4,128,2048]{2,1,0:T(8,128)(2,1)} %gather_fusion) | copy-start | bytes 6291460
  160.6 13.0 %copy-start.4 = (f32[128,512]{1,0:T(8,128)S(1)}, f32[128,512]{1,0:T(8,128)}, u32[]{:S(2)}) copy-start(f32[128,512]{1,0:T(8,128)} %shard_map.77) | copy-start | bytes 786436
  184.1 2.2 copy-start.1

commit v5 on v4

--- a/solution.py
+++ b/solution.py
@@ -85,7 +85,8 @@
     return sends
 
 
-def ring_sum_kernel(axis_names, axis, n, x_ref, out_ref, recv, acc, sems):
+def grad_ring_kernel(axis_names, axis, n, lt_ref, rt_ref, loss_ref, out_ref, loss_out, part, recv, acc,
+                     loss_slots, sems, loss_sems):
     me = lax.axis_index(axis)
 
     def dev_of(c):
@@ -95,32 +96,54 @@
     for d in range(1, n):
         pl.semaphore_signal(barrier, 1, device_id=dev_of((me + d) % n), device_id_type=MESH_ID)
     pl.semaphore_wait(barrier, n - 1)
-    half = x_ref.shape[1] // 2
+    loss_sends = gather_phase(n, me, dev_of, lambda c: loss_ref, lambda c: loss_slots.at[c],
+                              loss_sems.at[0], loss_sems.at[1])
+    blocks, width, _ = lt_ref.shape
+    rows = width // n
+    lane = rt_ref.shape[2]
+    for c in range(n):
+        for k in range(blocks):
+            part[c, :, pl.ds(k * lane, lane)] = jnp.dot(
+                lt_ref[k, pl.ds(c * rows, rows), :], rt_ref[k], preferred_element_type=jnp.float32
+            )
+    half = rows // 2
 
     def put(h, value):
         out_ref[pl.ds(h * half, half)] = value.astype(out_ref.dtype)
 
-    sends = ring_reduce_scatter(n, me, dev_of, x_ref, recv, acc, sems, put)
-    for cp in sends:
+    sends = ring_reduce_scatter(n, me, dev_of, part, recv, acc, sems, put)
+    total = loss_slots[0]
+    for s in range(1, n):
+        total = total + loss_slots[s]
+    loss_out[...] = total
+    for cp in sends + loss_sends:
         cp.wait_send()
 
 
-def ring_sum_scatter(x, axis_names, axis, n, cid, out_dtype):
-    _, rows, width = x.shape
+def grad_ring(lt, rt, loss_tile, axis_names, axis, n, cid):
+    blocks, width, _ = lt.shape
+    lane = rt.shape[2]
+    rows = width // n
+    cols = blocks * lane
+    f32 = jnp.float32
     return pl.pallas_call(
-        functools.partial(ring_sum_kernel, axis_names, axis, n),
-        out_shape=jax.ShapeDtypeStruct((rows, width), out_dtype),
-        in_specs=[pl.BlockSpec(memory_space=pltpu.VMEM)],
-        out_specs=pl.BlockSpec(memory_space=pltpu.VMEM),
+        functools.partial(grad_ring_kernel, axis_names, axis, n),
+        out_shape=(jax.ShapeDtypeStruct((rows, cols), jnp.bfloat16),
+                   jax.ShapeDtypeStruct(loss_tile.shape, f32)),
+        in_specs=[pl.BlockSpec(memory_space=pltpu.VMEM)] * 3,
+        out_specs=(pl.BlockSpec(memory_space=pltpu.VMEM), pl.BlockSpec(memory_space=pltpu.VMEM)),
         scratch_shapes=[
-            pltpu.VMEM((2, n - 1, rows // 2, width), x.dtype),
-            pltpu.VMEM((2, max(n - 2, 1), rows // 2, width), x.dtype),
+            pltpu.VMEM((n, rows, cols), f32),
+            pltpu.VMEM((2, n - 1, rows // 2, cols), f32),
+            pltpu.VMEM((2, max(n - 2, 1), rows // 2, cols), f32),
+            pltpu.VMEM((n,) + loss_tile.shape, f32),
             pltpu.SemaphoreType.DMA((2, 2, n - 1)),
+            pltpu.SemaphoreType.DMA((2, n)),
         ],
         compiler_params=pltpu.CompilerParams(
-            collective_id=cid, has_side_effects=True, vmem_limit_bytes=48 * 1024 * 1024
+            collective_id=cid, has_side_effects=True, vmem_limit_bytes=56 * 1024 * 1024
         ),
-    )(x)
+    )(lt, rt, loss_tile)
 
 
 def axis_sum_kernel(axis_names, axis, n, x_ref, out_ref, slots, send_sem, recv_sem):
@@ -401,24 +424,23 @@
     summed_rows = axis_sum(adjoint_rows, axis_names, "wid", 2, 2)
     g_act = summed_rows[:row_count]
     loss_tile = jnp.zeros((8, 128), jnp.float32).at[0, :LEVELS].set(summed_rows[row_count, :LEVELS])
-    total_sq = axis_sum(loss_tile, axis_names, "tok", lax.axis_size("tok"), 3)[0, :LEVELS]
-    level_losses = total_sq / (row_count * lax.axis_size("tok") * half_width * lax.axis_size("wid"))
     mask_full = jnp.broadcast_to(hits[:, :, None], (row_count, blocks_here, 128)).reshape(
         row_count, lat_count
     )
     _, pull = jax.vjp(gelu_tanh, pre)
     g_pre = pull(g_act * mask_full)[0].astype(jnp.bfloat16)
-    decode_term = jnp.einsum("ktd,tkc->dkc", err_half, act, preferred_element_type=jnp.float32)
-    encode_term = lax.dot_general(
-        resid, g_pre, (((0,), (0,)), ((), ())), preferred_element_type=jnp.float32
-    )
+    left = jnp.concatenate(
+        [err_half, jnp.broadcast_to(resid[None], (blocks_here, row_count, half_width))], axis=1
+    )
+    lt = jnp.transpose(left, (0, 2, 1))
+    right = jnp.concatenate(
+        [act.reshape(row_count, blocks_here, 128), g_pre.reshape(row_count, blocks_here, 128)], axis=0
+    )
+    rt = jnp.transpose(right, (1, 0, 2))
     tok_count = lax.axis_size("tok")
-    grad_share = ring_sum_scatter(
-        (decode_term.reshape(half_width, lat_count) + encode_term).reshape(
-            tok_count, half_width // tok_count, lat_count
-        ),
-        axis_names, "tok", tok_count, 4, jnp.bfloat16,
-    )
+    grad_share, loss_sum = grad_ring(lt, rt, loss_tile, axis_names, "tok", tok_count, 4)
+    total_sq = loss_sum[0, :LEVELS]
+    level_losses = total_sq / (row_count * tok_count * half_width * lax.axis_size("wid"))
     return (level_losses, grad_share)
 
 

time: 240 us -> 236 us (0.983)
  matrix products: 16.9 us -> 7.24 us
  other arithmetic: 7.43 us -> 14.6 us
    dot_general x2 -> x0, matrix products: 9.58 us -> none  [the longest x1 5.14 us: body(): lax.dot_general(resid, g_pre, (((0,), (0,)), ((), ())), preferred_element...]
    pallas_call x1, Pallas kernels: 39.5 us -> 47.2 us  [grad_ring(): pl.pallas_call(functools.partial(grad_ring_kernel, axis_names, axis, n),...]
    pallas_call x1, Pallas kernels: 129 us -> 123 us  [lat_sum(): pl.pallas_call(functools.partial(lat_sum_kernel, axis_names, ny, nlo, nhi...]
    add x1 -> x0, local copies, waits for them, and re-layouts: 5.34 us -> none  [body(): decode_term.reshape(half_width, lat_count) + encode_term]
    gather x1 -> x2, local copies, waits for them, and re-layouts: 3.59 us -> 7.55 us  [body(): err_half = jnp.take(cum_err, level_of, axis=0)]
    transpose x0 -> x2, other arithmetic: none -> 3.12 us  [the longest x1 2.39 us: body(): lt = jnp.transpose(left, (0, 2, 1))]
    pallas_call x3 -> x2, Pallas kernels: 26.1 us -> 24.1 us  [axis_sum(): pl.pallas_call(functools.partial(axis_sum_kernel, axis_names, axis, n), o...]
where the time goes in v5:
time: 236 us; the launch traced here: 233 us
  Pallas kernels  194 us (82%)
  local copies, waits for them, and re-layouts  15.6 us (7%)
  other arithmetic  14.6 us (6%)
  matrix products  7.24 us (3%)
    pallas_call x1, Pallas kernels, lat_sum(): pl.pallas_call(functools.partial(lat_sum_kernel, axis_names, ny, nlo, nhi...  123 us
    pallas_call x1, Pallas kernels, grad_ring(): pl.pallas_call(functools.partial(grad_ring_kernel, axis_names, axis, n),...  47.2 us
    pallas_call x2, Pallas kernels, axis_sum(): pl.pallas_call(functools.partial(axis_sum_kernel, axis_names, axis, n), o...  24.1 us
    gather x2, local copies, waits for them, and re-layouts, body(): err_half = jnp.take(cum_err, level_of, axis=0)  7.55 us

profile of v5, /device:TPU:1, one launch (start us, length us, event | category | flops | bytes accessed | tf_op | source)
XLA Modules:
  0.0 232.6 jit_solution(15508083616512831313)
XLA Ops:
  0.7 0.9 compare_reduce_fusion
  1.8 0.5 copy-done
  2.2 2.6 %fusion.22.x_ref = f32[128,512]{1,0:T(8,128)} fusion(bf16[128,2048]{1,0:T(8,128)(2,1)} %param.10, bf16[512,2048]{1,0:T(8,128)(2,1)S(1)} %copy-done), kind=kOutput, calls=%fused_computation.53 | convolution fusion | flops 268435456 | bytes 2883584 | tf_op jit(solution)/shard_map/dot_general | solution.py:386
  4.8 10.4 %shard_map.77 = f32[128,512]{1,0:T(8,128)} custom-call(f32[128,512]{1,0:T(8,128)} %fusion.22.x_ref), custom_call_target="tpu_custom_call" | custom-call | tf_op jit(solution)/shard_map/pallas_call | solution.py:169
  15.3 1.1 multiply_convert_fusion.1
  16.4 3.2 %fusion.x_ref = f32[4,128,2048]{2,1,0:T(8,128)} fusion(bf16[512,2048]{1,0:T(8,128)(2,1)S(1)} %copy-done, pred[4,512]{1,0:T(4,128)(4,1)S(1)} %broadcast_compare_fusion, bf16[128,512]{1,0:T(8,128)(2,1)S(1)} %get-tuple-element.32), kind=kOutput, calls=%fused_computation.5 | convolution fusion | flops 1074003968 | bytes 6424576 | tf_op jit(solution)/shard_map/dot_general | solution.py:401
  19.6 123.0 %shard_map.78 = f32[4,128,2048]{2,1,0:T(8,128)S(1)} custom-call(f32[4,128,2048]{2,1,0:T(8,128)} %fusion.x_ref), custom_call_target="tpu_custom_call" | custom-call | tf_op jit(solution)/shard_map/pallas_call | solution.py:352
  142.8 1.1 multiply_reduce_fusion
  143.9 0.4 fusion.2
  144.4 1.6 pad_maximum_fusion
  146.0 0.2 convert_reduce_fusion
  146.2 3.6 %gather_fusion = bf16[4,128,2048]{2,1,0:T(8,128)(2,1)} fusion(bf16[4,128,2048]{2,1,0:T(8,128)(2,1)} %pad_maximum_fusion, s32[1024]{0:T(1024)S(1)} %pad_clamp_fusion), kind=kCustom, calls=%fused_computation | custom fusion | bytes 4194320 | tf_op jit(solution)/shard_map/jit(_take)/gather | solution.py:418
  149.8 4.0 %copy.26 = bf16[4,128,2048]{1,2,0:T(8,128)(2,1)} copy(bf16[4,128,2048]{2,1,0:T(8,128)(2,1)} %gather_fusion) | data formatting | bytes 4194304 | tf_op jit(solution)/shard_map/jit(_take)/gather | solution.py:418
  153.7 1.9 broadcast_select_fusion
  155.6 1.4 fusion.23
  157.1 1.8 copy.36
  158.9 1.7 select_maximum_fusion.x_ref
  160.6 13.7 %shard_map.79 = f32[136,512]{1,0:T(8,128)} custom-call(f32[136,512]{1,0:T(8,128)} %select_maximum_fusion.x_ref), custom_call_target="tpu_custom_call" | custom-call | tf_op jit(solution)/shard_map/pallas_call | solution.py:169
  174.2 1.1 fusion.12
  175.5 0.1 copy.34
  175.8 0.1 copy.29
  175.9 0.1 multiply_convert_fusion
  176.1 0.7 maximum_bitcast_fusion.1.rt_ref
  176.8 0.7 slice.58
  177.5 0.6 scatter.9.loss_ref
  178.0 0.3 copy.27
  178.3 0.3 broadcast_in_dim.37
  178.6 1.3 copy-done.2
  179.9 2.4 %maximum_bitcast_fusion.lt_ref = bf16[4,2048,256]{2,1,0:T(8,128)(2,1)} fusion(bf16[4,128,2048]{1,2,0:T(8,128)(2,1)S(1)} %broadcast_in_dim.37, bf16[4,128,2048]{1,2,0:T(8,128)(2,1)S(1)} %copy-done.2), kind=kLoop, calls=%fused_computation.1 | loop fusion | flops 8388608 | bytes 8388608 | tf_op jit(solution)/shard_map/transpose | solution.py:435
  182.3 47.2 %shard_map.80 = (bf16[512,512]{1,0:T(8,128)(2,1)}, f32[8,128]{1,0:T(8,128)}) custom-call(bf16[4,2048,256]{2,1,0:T(8,128)(2,1)} %maximum_bitcast_fusion.lt_ref, bf16[4,256,128]{2,1,0:T(8,128)(2,1)} %maximum_bitcast_fusion.1.rt_ref, f32[8,128]{1,0:T(8,128)} %scatter.9.loss_ref), custom_call_target="tpu_custom_call" | custom-call | tf_op jit(solution)/shard_map/pallas_call | solution.py:129
  229.5 1.2 multiply_bitcast_fusion
  230.7 1.9 copy.39
  (27 shorter events, 0.7 us)
Async XLA Ops:
  0.6 1.6 copy-start
  1.6 13.7 %copy-start.5 = (f32[512]{0:T(512)S(1)}, f32[512]{0:T(512)}, u32[]{:S(2)}) copy-start(f32[512]{0:T(512)} %param.12) | copy-start | bytes 6148
  2.2 14.1 %copy-start.7 = (s32[4]{0:T(128)S(1)}, s32[4]{0:T(128)}, u32[]{:S(2)}) copy-start(s32[4]{0:T(128)} %param.15) | copy-start | bytes 52
  19.6 123.0 %copy-start.3 = (bf16[128,2048]{1,0:T(8,128)(2,1)S(1)}, bf16[128,2048]{1,0:T(8,128)(2,1)}, u32[]{:S(2)}) copy-start(bf16[128,2048]{1,0:T(8,128)(2,1)} %param.10) | copy-start | bytes 1572868
  19.6 123.2 %copy-start.6 = (f32[2048]{0:T(1024)S(1)}, f32[2048]{0:T(1024)}, u32[]{:S(2)}) copy-start(f32[2048]{0:T(1024)} %param.13) | copy-start | bytes 24580
  155.6 1.5 copy-start.1
  155.6 18.6 %copy-start.4 = (f32[128,512]{1,0:T(8,128)S(1)}, f32[128,512]{1,0:T(8,128)}, u32[]{:S(2)}) copy-start(f32[128,512]{1,0:T(8,128)} %shard_map.77) | copy-start | bytes 786436
  178.3 1.6 copy-start.2

commit v6 on v5

--- a/solution.py
+++ b/solution.py
@@ -101,17 +101,31 @@
     blocks, width, _ = lt_ref.shape
     rows = width // n
     lane = rt_ref.shape[2]
-    for c in range(n):
+
+    def make_chunk(c):
         for k in range(blocks):
             part[c, :, pl.ds(k * lane, lane)] = jnp.dot(
-                lt_ref[k, pl.ds(c * rows, rows), :], rt_ref[k], preferred_element_type=jnp.float32
+                lt_ref[k, pl.ds(pl.multiple_of(c * rows, rows), rows), :], rt_ref[k],
+                preferred_element_type=jnp.float32,
             )
+
+    first = sorted({(n - 1) % n, 1 % n})
+    later = [o for o in dict.fromkeys((2 % n, 0)) if o not in first]
+    for o in first:
+        make_chunk((me + o) % n)
     half = rows // 2
 
     def put(h, value):
         out_ref[pl.ds(h * half, half)] = value.astype(out_ref.dtype)
 
-    sends = ring_reduce_scatter(n, me, dev_of, part, recv, acc, sems, put)
+    sends = []
+    steps = ring_rs_steps(n, me, dev_of, part, recv, acc, sems, put, sends)
+    for i, (start, finish) in enumerate(steps):
+        start()
+        if i == 0:
+            for o in later:
+                make_chunk((me + o) % n)
+        finish()
     total = loss_slots[0]
     for s in range(1, n):
         total = total + loss_slots[s]
@@ -407,15 +421,12 @@
 
     errors = dec_bias[None, None, :] + levels - resid_full[None]
     squares = jnp.sum(errors * errors, axis=(1, 2))
-    running = errors[LEVELS - 1]
-    cum_list = [running]
+    level_of = jnp.sum((level_bounds[None, :] <= local_ids[:, None]).astype(jnp.int32), axis=1)
+    running = jnp.broadcast_to(errors[LEVELS - 1][None], (blocks_here, row_count, half_width))
     for level in range(LEVELS - 2, -1, -1):
-        running = running + errors[level]
-        cum_list.append(running)
-    cum_err = jnp.stack(cum_list[::-1]).astype(jnp.bfloat16)
-
-    level_of = jnp.sum((level_bounds[None, :] <= local_ids[:, None]).astype(jnp.int32), axis=1)
-    err_half = jnp.take(cum_err, level_of, axis=0)
+        used = (level >= level_of).astype(jnp.float32)[:, None, None]
+        running = running + used * errors[level][None]
+    err_half = running.astype(jnp.bfloat16)
     partial_adjoint = jnp.einsum(
         "ktd,kcd->tkc", err_half, dict_blocks, preferred_element_type=jnp.float32
     )

time: 236 us -> 241 us (1.021)
  local copies, waits for them, and re-layouts: 15.6 us -> 20.2 us
    mul x0 -> x3, local copies, waits for them, and re-layouts: none -> 7.64 us  [body(): running = running + used * errors[level][None]]
    gather x2 -> x0, local copies, waits for them, and re-layouts: 7.55 us -> none  [body(): err_half = jnp.take(cum_err, level_of, axis=0)]
    broadcast_in_dim x0 -> x2, local copies, waits for them, and re-layouts: none -> 4.65 us  [body(): jnp.broadcast_to(errors[LEVELS - 1][None], (blocks_here, row_count, half_...]
    pallas_call x1, Pallas kernels: 123 us -> 127 us  [lat_sum(): pl.pallas_call(functools.partial(lat_sum_kernel, axis_names, ny, nlo, nhi...]
    convert_element_type x0 -> x2, other arithmetic: none -> 3.19 us  [the longest x1 3.19 us: body(): err_half = running.astype(jnp.bfloat16)]
    pallas_call x1, Pallas kernels: 47.2 us -> 44.3 us  [grad_ring(): pl.pallas_call(functools.partial(grad_ring_kernel, axis_names, axis, n),...]
    pallas_call x2, Pallas kernels: 24.1 us -> 21.6 us  [axis_sum(): pl.pallas_call(functools.partial(axis_sum_kernel, axis_names, axis, n), o...]
where the time goes in v6:
time: 241 us; the launch traced here: 237 us
  Pallas kernels  193 us (80%)
  local copies, waits for them, and re-layouts  20.2 us (8%)
  other arithmetic  15.6 us (6%)
  matrix products  7.22 us (3%)
    pallas_call x1, Pallas kernels, lat_sum(): pl.pallas_call(functools.partial(lat_sum_kernel, axis_names, ny, nlo, nhi...  127 us
    pallas_call x1, Pallas kernels, grad_ring(): pl.pallas_call(functools.partial(grad_ring_kernel, axis_names, axis, n),...  44.3 us
    pallas_call x2, Pallas kernels, axis_sum(): pl.pallas_call(functools.partial(axis_sum_kernel, axis_names, axis, n), o...  21.6 us
    mul x3, local copies, waits for them, and re-layouts, body(): running = running + used * errors[level][None]  7.64 us

profile of v6, /device:TPU:1, one launch (start us, length us, event | category | flops | bytes accessed | tf_op | source)
XLA Modules:
  0.0 237.1 jit_solution(2579409731121431612)
XLA Ops:
  0.7 0.9 compare_reduce_fusion
  1.8 0.5 copy-done
  2.2 2.6 %fusion.18.x_ref = f32[128,512]{1,0:T(8,128)} fusion(bf16[128,2048]{1,0:T(8,128)(2,1)} %param.10, bf16[512,2048]{1,0:T(8,128)(2,1)S(1)} %copy-done), kind=kOutput, calls=%fused_computation.46 | convolution fusion | flops 268435456 | bytes 2883584 | tf_op jit(solution)/shard_map/dot_general | solution.py:400
  4.8 10.4 %shard_map.77 = f32[128,512]{1,0:T(8,128)} custom-call(f32[128,512]{1,0:T(8,128)} %fusion.18.x_ref), custom_call_target="tpu_custom_call" | custom-call | tf_op jit(solution)/shard_map/pallas_call | solution.py:183
  15.3 1.1 multiply_convert_fusion.1
  16.4 3.2 %fusion.x_ref = f32[4,128,2048]{2,1,0:T(8,128)} fusion(bf16[512,2048]{1,0:T(8,128)(2,1)S(1)} %copy-done, pred[4,512]{1,0:T(4,128)(4,1)S(1)} %broadcast_compare_fusion, bf16[128,512]{1,0:T(8,128)(2,1)S(1)} %get-tuple-element.32), kind=kOutput, calls=%fused_computation.4 | convolution fusion | flops 1074003968 | bytes 6424576 | tf_op jit(solution)/shard_map/dot_general | solution.py:415
  19.6 127.4 %shard_map.78 = f32[4,128,2048]{2,1,0:T(8,128)S(1)} custom-call(f32[4,128,2048]{2,1,0:T(8,128)} %fusion.x_ref), custom_call_target="tpu_custom_call" | custom-call | tf_op jit(solution)/shard_map/pallas_call | solution.py:366
  147.1 1.2 multiply_reduce_fusion
  148.3 2.1 slice_bitcast_fusion.3
  150.4 2.6 %copy.33 = f32[128,2048]{0,1:T(8,128)} copy(f32[128,2048]{1,0:T(8,128)} %get-tuple-element.34) | data formatting | bytes 2097152 | tf_op jit(solution)/shard_map/broadcast_in_dim | solution.py:425
  153.0 2.5 %copy.34 = f32[128,2048]{0,1:T(8,128)} copy(f32[128,2048]{1,0:T(8,128)} %get-tuple-element.37) | data formatting | bytes 2097152 | tf_op jit(solution)/shard_map/mul | solution.py:428
  155.5 2.5 %copy.35 = f32[128,2048]{0,1:T(8,128)} copy(f32[128,2048]{1,0:T(8,128)} %get-tuple-element.36) | data formatting | bytes 2097152 | tf_op jit(solution)/shard_map/mul | solution.py:428
  158.1 2.6 %copy.36 = f32[128,2048]{0,1:T(8,128)} copy(f32[128,2048]{1,0:T(8,128)} %get-tuple-element.35) | data formatting | bytes 2097152 | tf_op jit(solution)/shard_map/mul | solution.py:428
  160.6 0.2 convert_reduce_fusion
  160.8 3.2 %add_convert_fusion = bf16[4,128,2048]{1,2,0:T(8,128)(2,1)S(1)} fusion(f32[128,2048]{0,1:T(8,128)} %copy.36, f32[4]{0:T(128)S(1)} %get-tuple-element.39, f32[128,2048]{0,1:T(8,128)} %copy.35, f32[4]{0:T(128)S(1)} %get-tuple-element.40, f32[128,2048]{0,1:T(8,128)} %copy.34, f32[4]{0:T(128)S(1)} %get-tuple-element.38, f32[128,2048]{0,1:T(8,128)} %copy.33), kind=kLoop, calls=%fused_computation.2 | loop fusion | flops 7340032 | bytes 6291504 | tf_op jit(solution)/shard_map/convert_element_type | solution.py:429
  164.0 1.3 copy-done.1
  165.3 1.4 fusion.19
  166.8 1.8 copy.46
  168.5 1.7 select_maximum_fusion.x_ref
  170.2 11.1 %shard_map.79 = f32[136,512]{1,0:T(8,128)} custom-call(f32[136,512]{1,0:T(8,128)} %select_maximum_fusion.x_ref), custom_call_target="tpu_custom_call" | custom-call | tf_op jit(solution)/shard_map/pallas_call | solution.py:183
  181.4 1.1 fusion.10
  182.6 0.1 copy.44
  182.9 0.1 copy.39
  183.2 0.7 maximum_bitcast_fusion.1.rt_ref
  183.9 0.7 slice.58
  184.6 0.6 scatter.9.loss_ref
  185.2 0.3 copy.37
  185.5 0.3 broadcast_in_dim.31
  185.8 4.0 %maximum_bitcast_fusion.lt_ref = bf16[4,2048,256]{2,1,0:T(8,128)(2,1)} fusion(bf16[4,128,2048]{1,2,0:T(8,128)(2,1)S(1)} %broadcast_in_dim.31, bf16[4,128,2048]{1,2,0:T(8,128)(2,1)} %copy-done.1), kind=kLoop, calls=%fused_computation | loop fusion | flops 8388608 | bytes 8388608 | tf_op jit(solution)/shard_map/transpose | solution.py:446
  189.7 44.3 %shard_map.80 = (bf16[512,512]{1,0:T(8,128)(2,1)}, f32[8,128]{1,0:T(8,128)}) custom-call(bf16[4,2048,256]{2,1,0:T(8,128)(2,1)} %maximum_bitcast_fusion.lt_ref, bf16[4,256,128]{2,1,0:T(8,128)(2,1)} %maximum_bitcast_fusion.1.rt_ref, f32[8,128]{1,0:T(8,128)} %scatter.9.loss_ref), custom_call_target="tpu_custom_call" | custom-call | tf_op jit(solution)/shard_map/pallas_call | solution.py:143
  234.1 1.2 multiply_bitcast_fusion
  235.3 1.9 copy.49
  (23 shorter events, 0.7 us)
Async XLA Ops:
  0.6 1.6 copy-start
  0.6 14.6 %copy-start.4 = (f32[512]{0:T(512)S(1)}, f32[512]{0:T(512)}, u32[]{:S(2)}) copy-start(f32[512]{0:T(512)} %param.12) | copy-start | bytes 6148
  0.7 15.7 %copy-start.6 = (s32[4]{0:T(128)S(1)}, s32[4]{0:T(128)}, u32[]{:S(2)}) copy-start(s32[4]{0:T(128)} %param.15) | copy-start | bytes 52
  19.6 127.4 %copy-start.2 = (bf16[128,2048]{1,0:T(8,128)(2,1)S(1)}, bf16[128,2048]{1,0:T(8,128)(2,1)}, u32[]{:S(2)}) copy-start(bf16[128,2048]{1,0:T(8,128)(2,1)} %param.10) | copy-start | bytes 1572868
  19.6 127.5 %copy-start.5 = (f32[2048]{0:T(1024)S(1)}, f32[2048]{0:T(1024)}, u32[]{:S(2)}) copy-start(f32[2048]{0:T(1024)} %param.13) | copy-start | bytes 24580
  164.0 1.3 copy-start.1
  164.0 17.3 %copy-start.3 = (f32[128,512]{1,0:T(8,128)S(1)}, f32[128,512]{1,0:T(8,128)}, u32[]{:S(2)}) copy-start(f32[128,512]{1,0:T(8,128)} %shard_map.77) | copy-start | bytes 786436

commit v7 on v6

--- a/solution.py
+++ b/solution.py
@@ -421,12 +421,15 @@
 
     errors = dec_bias[None, None, :] + levels - resid_full[None]
     squares = jnp.sum(errors * errors, axis=(1, 2))
+    running = errors[LEVELS - 1]
+    cum_list = [running]
+    for level in range(LEVELS - 2, -1, -1):
+        running = running + errors[level]
+        cum_list.append(running)
+    cum_err = jnp.stack(cum_list[::-1]).astype(jnp.bfloat16)
+
     level_of = jnp.sum((level_bounds[None, :] <= local_ids[:, None]).astype(jnp.int32), axis=1)
-    running = jnp.broadcast_to(errors[LEVELS - 1][None], (blocks_here, row_count, half_width))
-    for level in range(LEVELS - 2, -1, -1):
-        used = (level >= level_of).astype(jnp.float32)[:, None, None]
-        running = running + used * errors[level][None]
-    err_half = running.astype(jnp.bfloat16)
+    err_half = jnp.take(cum_err, level_of, axis=0)
     partial_adjoint = jnp.einsum(
         "ktd,kcd->tkc", err_half, dict_blocks, preferred_element_type=jnp.float32
     )

time: 241 us -> 236 us (0.979)
  local copies, waits for them, and re-layouts: 20.2 us -> 15.6 us
    mul x3 -> x0, local copies, waits for them, and re-layouts: 7.64 us -> none  [body(): running = running + used * errors[level][None]]
    gather x0 -> x2, local copies, waits for them, and re-layouts: none -> 7.55 us  [body(): err_half = jnp.take(cum_err, level_of, axis=0)]
    broadcast_in_dim x2 -> x0, local copies, waits for them, and re-layouts: 4.65 us -> none  [body(): jnp.broadcast_to(errors[LEVELS - 1][None], (blocks_here, row_count, half_...]
    pallas_call x1, Pallas kernels: 127 us -> 123 us  [lat_sum(): pl.pallas_call(functools.partial(lat_sum_kernel, axis_names, ny, nlo, nhi...]
    convert_element_type x2 -> x0, other arithmetic: 3.19 us -> none  [the longest x1 3.19 us: body(): err_half = running.astype(jnp.bfloat16)]
    pallas_call x2, Pallas kernels: 21.6 us -> 24.1 us  [axis_sum(): pl.pallas_call(functools.partial(axis_sum_kernel, axis_names, axis, n), o...]
where the time goes in v7:
time: 236 us; the launch traced here: 232 us
  Pallas kernels  194 us (82%)
  local copies, waits for them, and re-layouts  15.6 us (7%)
  other arithmetic  14.6 us (6%)
  matrix products  7.24 us (3%)
    pallas_call x1, Pallas kernels, lat_sum(): pl.pallas_call(functools.partial(lat_sum_kernel, axis_names, ny, nlo, nhi...  123 us
    pallas_call x1, Pallas kernels, grad_ring(): pl.pallas_call(functools.partial(grad_ring_kernel, axis_names, axis, n),...  46.7 us
    pallas_call x2, Pallas kernels, axis_sum(): pl.pallas_call(functools.partial(axis_sum_kernel, axis_names, axis, n), o...  24.1 us
    gather x2, local copies, waits for them, and re-layouts, body(): err_half = jnp.take(cum_err, level_of, axis=0)  7.55 us

profile of v7, /device:TPU:1, one launch (start us, length us, event | category | flops | bytes accessed | tf_op | source)
XLA Modules:
  0.0 232.1 jit_solution(4874016322710549206)
XLA Ops:
  0.7 0.9 compare_reduce_fusion
  1.8 0.5 copy-done
  2.2 2.6 %fusion.22.x_ref = f32[128,512]{1,0:T(8,128)} fusion(bf16[128,2048]{1,0:T(8,128)(2,1)} %param.10, bf16[512,2048]{1,0:T(8,128)(2,1)S(1)} %copy-done), kind=kOutput, calls=%fused_computation.53 | convolution fusion | flops 268435456 | bytes 2883584 | tf_op jit(solution)/shard_map/dot_general | solution.py:400
  4.8 10.4 %shard_map.77 = f32[128,512]{1,0:T(8,128)} custom-call(f32[128,512]{1,0:T(8,128)} %fusion.22.x_ref), custom_call_target="tpu_custom_call" | custom-call | tf_op jit(solution)/shard_map/pallas_call | solution.py:183
  15.3 1.1 multiply_convert_fusion.1
  16.4 3.2 %fusion.x_ref = f32[4,128,2048]{2,1,0:T(8,128)} fusion(bf16[512,2048]{1,0:T(8,128)(2,1)S(1)} %copy-done, pred[4,512]{1,0:T(4,128)(4,1)S(1)} %broadcast_compare_fusion, bf16[128,512]{1,0:T(8,128)(2,1)S(1)} %get-tuple-element.32), kind=kOutput, calls=%fused_computation.5 | convolution fusion | flops 1074003968 | bytes 6424576 | tf_op jit(solution)/shard_map/dot_general | solution.py:415
  19.6 123.0 %shard_map.78 = f32[4,128,2048]{2,1,0:T(8,128)S(1)} custom-call(f32[4,128,2048]{2,1,0:T(8,128)} %fusion.x_ref), custom_call_target="tpu_custom_call" | custom-call | tf_op jit(solution)/shard_map/pallas_call | solution.py:366
  142.8 1.1 multiply_reduce_fusion
  143.9 0.4 fusion.2
  144.4 1.6 pad_maximum_fusion
  146.0 0.2 convert_reduce_fusion
  146.2 3.6 %gather_fusion = bf16[4,128,2048]{2,1,0:T(8,128)(2,1)} fusion(bf16[4,128,2048]{2,1,0:T(8,128)(2,1)} %pad_maximum_fusion, s32[1024]{0:T(1024)S(1)} %pad_clamp_fusion), kind=kCustom, calls=%fused_computation | custom fusion | bytes 4194320 | tf_op jit(solution)/shard_map/jit(_take)/gather | solution.py:432
  149.8 4.0 %copy.26 = bf16[4,128,2048]{1,2,0:T(8,128)(2,1)} copy(bf16[4,128,2048]{2,1,0:T(8,128)(2,1)} %gather_fusion) | data formatting | bytes 4194304 | tf_op jit(solution)/shard_map/jit(_take)/gather | solution.py:432
  153.7 1.9 broadcast_select_fusion
  155.6 1.4 fusion.23
  157.1 1.8 copy.36
  158.9 1.7 select_maximum_fusion.x_ref
  160.6 13.7 %shard_map.79 = f32[136,512]{1,0:T(8,128)} custom-call(f32[136,512]{1,0:T(8,128)} %select_maximum_fusion.x_ref), custom_call_target="tpu_custom_call" | custom-call | tf_op jit(solution)/shard_map/pallas_call | solution.py:183
  174.2 1.1 fusion.12
  175.5 0.1 copy.34
  175.8 0.1 copy.29
  175.9 0.1 multiply_convert_fusion
  176.1 0.7 maximum_bitcast_fusion.1.rt_ref
  176.8 0.7 slice.58
  177.5 0.6 scatter.9.loss_ref
  178.0 0.3 copy.27
  178.3 0.3 broadcast_in_dim.37
  178.6 1.3 copy-done.2
  179.9 2.4 %maximum_bitcast_fusion.lt_ref = bf16[4,2048,256]{2,1,0:T(8,128)(2,1)} fusion(bf16[4,128,2048]{1,2,0:T(8,128)(2,1)S(1)} %broadcast_in_dim.37, bf16[4,128,2048]{1,2,0:T(8,128)(2,1)S(1)} %copy-done.2), kind=kLoop, calls=%fused_computation.1 | loop fusion | flops 8388608 | bytes 8388608 | tf_op jit(solution)/shard_map/transpose | solution.py:449
  182.3 46.7 %shard_map.80 = (bf16[512,512]{1,0:T(8,128)(2,1)}, f32[8,128]{1,0:T(8,128)}) custom-call(bf16[4,2048,256]{2,1,0:T(8,128)(2,1)} %maximum_bitcast_fusion.lt_ref, bf16[4,256,128]{2,1,0:T(8,128)(2,1)} %maximum_bitcast_fusion.1.rt_ref, f32[8,128]{1,0:T(8,128)} %scatter.9.loss_ref), custom_call_target="tpu_custom_call" | custom-call | tf_op jit(solution)/shard_map/pallas_call | solution.py:143
  229.0 1.2 multiply_bitcast_fusion
  230.2 1.9 copy.39
  (27 shorter events, 0.7 us)
Async XLA Ops:
  0.6 1.6 copy-start
  1.6 13.7 %copy-start.5 = (f32[512]{0:T(512)S(1)}, f32[512]{0:T(512)}, u32[]{:S(2)}) copy-start(f32[512]{0:T(512)} %param.12) | copy-start | bytes 6148
  2.2 14.1 %copy-start.7 = (s32[4]{0:T(128)S(1)}, s32[4]{0:T(128)}, u32[]{:S(2)}) copy-start(s32[4]{0:T(128)} %param.15) | copy-start | bytes 52
  19.6 123.0 %copy-start.3 = (bf16[128,2048]{1,0:T(8,128)(2,1)S(1)}, bf16[128,2048]{1,0:T(8,128)(2,1)}, u32[]{:S(2)}) copy-start(bf16[128,2048]{1,0:T(8,128)(2,1)} %param.10) | copy-start | bytes 1572868
  19.6 123.2 %copy-start.6 = (f32[2048]{0:T(1024)S(1)}, f32[2048]{0:T(1024)}, u32[]{:S(2)}) copy-start(f32[2048]{0:T(1024)} %param.13) | copy-start | bytes 24580
  155.6 1.5 copy-start.1
  155.6 18.6 %copy-start.4 = (f32[128,512]{1,0:T(8,128)S(1)}, f32[128,512]{1,0:T(8,128)}, u32[]{:S(2)}) copy-start(f32[128,512]{1,0:T(8,128)} %shard_map.77) | copy-start | bytes 786436
  178.3 1.6 copy-start.2

commit v8 on v7

--- a/solution.py
+++ b/solution.py
@@ -409,14 +409,12 @@
     )
     act_flat = act.reshape(row_count, lat_count)
 
-    latent_block = first_block + jnp.arange(lat_count, dtype=jnp.int32) // 128
-    keep = latent_block[None, :] < level_bounds[:, None]
-    act_stack = jnp.where(keep[:, None, :], act_flat[None], jnp.zeros((), jnp.bfloat16))
-    contrib = jnp.dot(
-        act_stack.reshape(LEVELS * row_count, lat_count),
-        dictionary,
+    per_block = jnp.einsum(
+        "tkc,kcd->ktd", act.reshape(row_count, blocks_here, 128), dict_blocks,
         preferred_element_type=jnp.float32,
-    ).reshape(LEVELS, row_count, half_width)
+    )
+    keep = (local_ids[None, :] < level_bounds[:, None]).astype(jnp.float32)
+    contrib = jnp.sum(keep[:, :, None, None] * per_block[None], axis=1)
     levels = lat_sum(contrib, axis_names, n_lat, 0)
 
     errors = dec_bias[None, None, :] + levels - resid_full[None]

time: 236 us -> 233 us (0.987)
  the two profiles are of different devices: /device:TPU:1 before, /device:TPU:40 now
where the time goes in v8:
time: 233 us
  Pallas kernels  196 us (84%)
  other arithmetic  16.9 us (7%)
  local copies, waits for them, and re-layouts  14.7 us (6%)
  matrix products  4.01 us (2%)
    pallas_call x1, Pallas kernels, lat_sum(): pl.pallas_call(functools.partial(lat_sum_kernel, axis_names, ny, nlo, nhi...  140 us
    pallas_call x1, Pallas kernels, grad_ring(): pl.pallas_call(functools.partial(grad_ring_kernel, axis_names, axis, n),...  48.2 us
    pallas_call x2, Pallas kernels, axis_sum(): pl.pallas_call(functools.partial(axis_sum_kernel, axis_names, axis, n), o...  7.93 us
    gather x2, local copies, waits for them, and re-layouts, body(): err_half = jnp.take(cum_err, level_of, axis=0)  7.55 us
    unnamed x18, local copies, waits for them, and re-layouts  4.72 us

profile of v8, /device:TPU:40, one launch (start us, length us, event | category | flops | bytes accessed | tf_op | source)
XLA Modules:
  0.0 232.7 jit_solution(914296389892960938)
XLA Ops:
  0.7 0.9 compare_reduce_fusion
  1.6 0.6 copy-done
  2.2 2.6 %fusion.11.x_ref = f32[128,512]{1,0:T(8,128)} fusion(bf16[128,2048]{1,0:T(8,128)(2,1)} %param.10, bf16[512,2048]{1,0:T(8,128)(2,1)S(1)} %copy-done), kind=kOutput, calls=%fused_computation.38 | convolution fusion | flops 268435456 | bytes 2883584 | tf_op jit(solution)/shard_map/dot_general | solution.py:400
  4.8 3.9 %shard_map.77 = f32[128,512]{1,0:T(8,128)} custom-call(f32[128,512]{1,0:T(8,128)} %fusion.11.x_ref), custom_call_target="tpu_custom_call" | custom-call | tf_op jit(solution)/shard_map/pallas_call | solution.py:183
  8.8 1.0 multiply_multiply_fusion.2
  9.9 0.1 copy.24
  10.2 0.7 fusion.12
  11.0 3.3 %multiply_reduce_fusion.x_ref = f32[4,128,2048]{2,1,0:T(8,128)} fusion(f32[4,128,2048]{2,1,0:T(8,128)S(1)} %fusion.12, f32[4,4]{1,0:T(4,128)S(1)} %compare_convert_fusion), kind=kLoop, calls=%fused_computation.1 | loop fusion | flops 7340032 | bytes 8388672 | tf_op jit(solution)/shard_map/reduce_sum | solution.py:417
  14.3 140.1 %shard_map.78 = f32[4,128,2048]{2,1,0:T(8,128)S(1)} custom-call(f32[4,128,2048]{2,1,0:T(8,128)} %multiply_reduce_fusion.x_ref), custom_call_target="tpu_custom_call" | custom-call | tf_op jit(solution)/shard_map/pallas_call | solution.py:366
  154.5 1.1 multiply_reduce_fusion.1
  155.7 0.4 fusion
  156.2 1.6 pad_maximum_fusion
  157.7 0.2 convert_reduce_fusion
  157.9 3.6 %gather_fusion = bf16[4,128,2048]{2,1,0:T(8,128)(2,1)} fusion(bf16[4,128,2048]{2,1,0:T(8,128)(2,1)} %pad_maximum_fusion, s32[1024]{0:T(1024)S(1)} %pad_clamp_fusion), kind=kCustom, calls=%fused_computation | custom fusion | bytes 4194320 | tf_op jit(solution)/shard_map/jit(_take)/gather | solution.py:430
  161.6 3.9 %copy.25 = bf16[4,128,2048]{1,2,0:T(8,128)(2,1)} copy(bf16[4,128,2048]{2,1,0:T(8,128)(2,1)} %gather_fusion) | data formatting | bytes 4194304 | tf_op jit(solution)/shard_map/jit(_take)/gather | solution.py:430
  165.5 1.9 broadcast_select_fusion
  167.4 0.7 fusion.13
  168.1 0.6 copy-done.1
  168.8 0.7 select_maximum_fusion.x_ref
  169.6 4.0 %shard_map.79 = f32[136,512]{1,0:T(8,128)} custom-call(f32[136,512]{1,0:T(8,128)} %select_maximum_fusion.x_ref), custom_call_target="tpu_custom_call" | custom-call | tf_op jit(solution)/shard_map/pallas_call | solution.py:183
  173.8 1.1 fusion.8
  175.0 0.1 copy.32
  175.2 0.7 maximum_bitcast_fusion.1.rt_ref
  175.9 0.7 slice.58
  176.6 0.6 scatter.9.loss_ref
  177.2 0.3 copy.26
  177.5 0.3 broadcast_in_dim.11
  177.7 1.3 copy-done.2
  179.0 2.4 %maximum_bitcast_fusion.lt_ref = bf16[4,2048,256]{2,1,0:T(8,128)(2,1)} fusion(bf16[4,128,2048]{1,2,0:T(8,128)(2,1)S(1)} %broadcast_in_dim.11, bf16[4,128,2048]{1,2,0:T(8,128)(2,1)S(1)} %copy-done.2), kind=kLoop, calls=%fused_computation.2 | loop fusion | flops 8388608 | bytes 8388608 | tf_op jit(solution)/shard_map/transpose | solution.py:447
  181.4 48.2 %shard_map.80 = (bf16[512,512]{1,0:T(8,128)(2,1)}, f32[8,128]{1,0:T(8,128)}) custom-call(bf16[4,2048,256]{2,1,0:T(8,128)(2,1)} %maximum_bitcast_fusion.lt_ref, bf16[4,256,128]{2,1,0:T(8,128)(2,1)} %maximum_bitcast_fusion.1.rt_ref, f32[8,128]{1,0:T(8,128)} %scatter.9.loss_ref), custom_call_target="tpu_custom_call" | custom-call | tf_op jit(solution)/shard_map/pallas_call | solution.py:143
  229.7 1.2 multiply_bitcast_fusion
  230.8 1.9 copy.37
  (27 shorter events, 0.9 us)
Async XLA Ops:
  0.6 1.6 copy-start
  0.6 8.1 %copy-start.5 = (f32[512]{0:T(512)S(1)}, f32[512]{0:T(512)}, u32[]{:S(2)}) copy-start(f32[512]{0:T(512)} %param.12) | copy-start | bytes 6148
  10.2 0.7 copy-start.7
  14.3 140.1 %copy-start.3 = (bf16[128,2048]{1,0:T(8,128)(2,1)S(1)}, bf16[128,2048]{1,0:T(8,128)(2,1)}, u32[]{:S(2)}) copy-start(bf16[128,2048]{1,0:T(8,128)(2,1)} %param.10) | copy-start | bytes 1572868
  14.3 140.2 %copy-start.6 = (f32[2048]{0:T(1024)S(1)}, f32[2048]{0:T(1024)}, u32[]{:S(2)}) copy-start(f32[2048]{0:T(1024)} %param.13) | copy-start | bytes 24580
  167.3 1.4 copy-start.1
  168.7 5.0 %copy-start.4 = (f32[128,512]{1,0:T(8,128)S(1)}, f32[128,512]{1,0:T(8,128)}, u32[]{:S(2)}) copy-start(f32[128,512]{1,0:T(8,128)} %shard_map.77) | copy-start | bytes 786436
  177.4 1.6 copy-start.2

commit v9 on v8

--- a/solution.py
+++ b/solution.py
@@ -335,7 +335,7 @@
         steps += ring_ag_steps(ny, my_y, y_dev, ag1.at[q], out_ref.at[:, :, width], ring_sems.at[q, 1], sends)
         streams.append(steps)
 
-    lag = ny - 1
+    lag = ny
     total_slots = len(streams[0]) + lag
     for slot in range(total_slots):
         active = []

time: 233 us -> 235 us (level)
  the two profiles are of different devices: /device:TPU:40 before, /device:TPU:1 now
where the time goes in v9:
time: 235 us; the launch traced here: 231 us
  Pallas kernels  194 us (83%)
  other arithmetic  16.9 us (7%)
  local copies, waits for them, and re-layouts  14.7 us (6%)
  matrix products  4.01 us (2%)
    pallas_call x1, Pallas kernels, lat_sum(): pl.pallas_call(functools.partial(lat_sum_kernel, axis_names, ny, nlo, nhi...  125 us
    pallas_call x1, Pallas kernels, grad_ring(): pl.pallas_call(functools.partial(grad_ring_kernel, axis_names, axis, n),...  43 us
    pallas_call x2, Pallas kernels, axis_sum(): pl.pallas_call(functools.partial(axis_sum_kernel, axis_names, axis, n), o...  26.4 us
    gather x2, local copies, waits for them, and re-layouts, body(): err_half = jnp.take(cum_err, level_of, axis=0)  7.55 us
    unnamed x18, local copies, waits for them, and re-layouts  4.72 us

profile of v9, /device:TPU:1, one launch (start us, length us, event | category | flops | bytes accessed | tf_op | source)
XLA Modules:
  0.0 230.9 jit_solution(920793238679567724)
XLA Ops:
  0.7 0.9 compare_reduce_fusion
  1.6 0.6 copy-done
  2.2 2.6 %fusion.11.x_ref = f32[128,512]{1,0:T(8,128)} fusion(bf16[128,2048]{1,0:T(8,128)(2,1)} %param.10, bf16[512,2048]{1,0:T(8,128)(2,1)S(1)} %copy-done), kind=kOutput, calls=%fused_computation.38 | convolution fusion | flops 268435456 | bytes 2883584 | tf_op jit(solution)/shard_map/dot_general | solution.py:400
  4.8 10.4 %shard_map.77 = f32[128,512]{1,0:T(8,128)} custom-call(f32[128,512]{1,0:T(8,128)} %fusion.11.x_ref), custom_call_target="tpu_custom_call" | custom-call | tf_op jit(solution)/shard_map/pallas_call | solution.py:183
  15.2 1.0 multiply_multiply_fusion.2
  16.4 0.1 copy.24
  16.7 0.7 fusion.12
  17.5 3.3 %multiply_reduce_fusion.x_ref = f32[4,128,2048]{2,1,0:T(8,128)} fusion(f32[4,128,2048]{2,1,0:T(8,128)S(1)} %fusion.12, f32[4,4]{1,0:T(4,128)S(1)} %compare_convert_fusion), kind=kLoop, calls=%fused_computation.1 | loop fusion | flops 7340032 | bytes 8388672 | tf_op jit(solution)/shard_map/reduce_sum | solution.py:417
  20.8 125.1 %shard_map.78 = f32[4,128,2048]{2,1,0:T(8,128)S(1)} custom-call(f32[4,128,2048]{2,1,0:T(8,128)} %multiply_reduce_fusion.x_ref), custom_call_target="tpu_custom_call" | custom-call | tf_op jit(solution)/shard_map/pallas_call | solution.py:366
  146.1 1.1 multiply_reduce_fusion.1
  147.2 0.4 fusion
  147.7 1.6 pad_maximum_fusion
  149.2 0.2 convert_reduce_fusion
  149.4 3.6 %gather_fusion = bf16[4,128,2048]{2,1,0:T(8,128)(2,1)} fusion(bf16[4,128,2048]{2,1,0:T(8,128)(2,1)} %pad_maximum_fusion, s32[1024]{0:T(1024)S(1)} %pad_clamp_fusion), kind=kCustom, calls=%fused_computation | custom fusion | bytes 4194320 | tf_op jit(solution)/shard_map/jit(_take)/gather | solution.py:430
  153.1 3.9 %copy.25 = bf16[4,128,2048]{1,2,0:T(8,128)(2,1)} copy(bf16[4,128,2048]{2,1,0:T(8,128)(2,1)} %gather_fusion) | data formatting | bytes 4194304 | tf_op jit(solution)/shard_map/jit(_take)/gather | solution.py:430
  157.0 1.9 broadcast_select_fusion
  158.9 0.7 fusion.13
  159.6 0.6 copy-done.1
  160.3 0.7 select_maximum_fusion.x_ref
  161.1 16.0 %shard_map.79 = f32[136,512]{1,0:T(8,128)} custom-call(f32[136,512]{1,0:T(8,128)} %select_maximum_fusion.x_ref), custom_call_target="tpu_custom_call" | custom-call | tf_op jit(solution)/shard_map/pallas_call | solution.py:183
  177.2 1.1 fusion.8
  178.5 0.1 copy.32
  178.6 0.7 maximum_bitcast_fusion.1.rt_ref
  179.4 0.7 slice.58
  180.0 0.6 scatter.9.loss_ref
  180.6 0.3 copy.26
  180.9 0.3 broadcast_in_dim.11
  181.2 1.3 copy-done.2
  182.5 2.4 %maximum_bitcast_fusion.lt_ref = bf16[4,2048,256]{2,1,0:T(8,128)(2,1)} fusion(bf16[4,128,2048]{1,2,0:T(8,128)(2,1)S(1)} %broadcast_in_dim.11, bf16[4,128,2048]{1,2,0:T(8,128)(2,1)S(1)} %copy-done.2), kind=kLoop, calls=%fused_computation.2 | loop fusion | flops 8388608 | bytes 8388608 | tf_op jit(solution)/shard_map/transpose | solution.py:447
  184.9 43.0 %shard_map.80 = (bf16[512,512]{1,0:T(8,128)(2,1)}, f32[8,128]{1,0:T(8,128)}) custom-call(bf16[4,2048,256]{2,1,0:T(8,128)(2,1)} %maximum_bitcast_fusion.lt_ref, bf16[4,256,128]{2,1,0:T(8,128)(2,1)} %maximum_bitcast_fusion.1.rt_ref, f32[8,128]{1,0:T(8,128)} %scatter.9.loss_ref), custom_call_target="tpu_custom_call" | custom-call | tf_op jit(solution)/shard_map/pallas_call | solution.py:143
  227.9 1.2 multiply_bitcast_fusion
  229.1 1.9 copy.37
  (27 shorter events, 0.9 us)
Async XLA Ops:
  0.6 1.6 copy-start
  0.6 14.6 %copy-start.5 = (f32[512]{0:T(512)S(1)}, f32[512]{0:T(512)}, u32[]{:S(2)}) copy-start(f32[512]{0:T(512)} %param.12) | copy-start | bytes 6148
  16.7 0.7 copy-start.7
  20.8 125.1 %copy-start.3 = (bf16[128,2048]{1,0:T(8,128)(2,1)S(1)}, bf16[128,2048]{1,0:T(8,128)(2,1)}, u32[]{:S(2)}) copy-start(bf16[128,2048]{1,0:T(8,128)(2,1)} %param.10) | copy-start | bytes 1572868
  20.8 125.2 %copy-start.6 = (f32[2048]{0:T(1024)S(1)}, f32[2048]{0:T(1024)}, u32[]{:S(2)}) copy-start(f32[2048]{0:T(1024)} %param.13) | copy-start | bytes 24580
  158.9 1.4 copy-start.1
  160.2 17.0 %copy-start.4 = (f32[128,512]{1,0:T(8,128)S(1)}, f32[128,512]{1,0:T(8,128)}, u32[]{:S(2)}) copy-start(f32[128,512]{1,0:T(8,128)} %shard_map.77) | copy-start | bytes 786436
  180.9 1.6 copy-start.2
